TPU v7x, 32 devices: a whole 2x2x4 slice. The times are simulated.
32 devices in a mesh: ctx: 4 (over x, core), exp: 8 (over z, y).
Axes of the slice: x: 2, y: 2, z: 4, core: 2. Of those that a mesh axis runs over, the one named last changes fastest.
Arguments:
- inputs: bfloat16 [8, 1536, 768], P('exp', 'ctx'), may hold values from -6 to 6
- segments: int32 [8, 1536], P('exp', 'ctx'), may hold values from 0 to 15, as said below
- routes: int32 [8, 1536, 1], P('exp', 'ctx'), may hold values from 0 to 7; in each aligned block of 384 rows (0 to 383, 384 to 767, ..., all dimensions but the last counted through in order) at most 60 rows name the same one
- cotangent: bfloat16 [8, 1536, 768], P('exp', 'ctx'), may hold values from -6 to 6
- norm_gain: bfloat16 [768], P(('ctx', 'exp')), may hold values from 0.5 to 1.5
- in_proj: bfloat16 [768, 3072], P(('ctx', 'exp')), may hold values from -0.21875 to 0.21875
- conv_taps: bfloat16 [1536, 4], P(('ctx', 'exp')), may hold values from -3 to 3
- conv_bias: bfloat16 [1536], P(('ctx', 'exp')), may hold values from -1.5 to 1.5
- x_proj: bfloat16 [1536, 80], P(('ctx', 'exp')), may hold values from -0.15625 to 0.15625
- dt_proj: bfloat16 [48, 1536], P(None, ('ctx', 'exp')), may hold values from -0.875 to 0.875
- dt_bias: bfloat16 [1536], P(('ctx', 'exp')), may hold values from -5.5 to -3.5
- log_decay: bfloat16 [1536, 16], P(('ctx', 'exp')), may hold values from -4 to 1.1953125
- skip_gain: bfloat16 [1536], P(('ctx', 'exp')), may hold values from 0.5 to 1.5
- out_proj: bfloat16 [1536, 768], P(('ctx', 'exp')), may hold values from -0.3125 to 0.3125
- moe_gain: bfloat16 [768], P(('ctx', 'exp')), may hold values from 0.5 to 1.5
- router: bfloat16 [768, 8], P(('ctx', 'exp')), may hold values from -0.15625 to 0.15625
- expert_in: bfloat16 [8, 768, 3072], P('exp', None, 'ctx'), may hold values from -0.21875 to 0.21875
- expert_out: bfloat16 [8, 3072, 768], P('exp', 'ctx'), may hold values from -0.875 to 0.875
Outputs:
- outputs: bfloat16 [8, 1536, 768], P('exp', 'ctx')
- grad_inputs: float32 [8, 1536, 768], P('exp', 'ctx')
- grad_norm_gain: float32 [768], P(('ctx', 'exp'))
- grad_in_proj: float32 [768, 3072], P(('ctx', 'exp'))
- grad_conv_taps: float32 [1536, 4], P(('ctx', 'exp'))
- grad_conv_bias: float32 [1536], P(('ctx', 'exp'))
- grad_x_proj: float32 [1536, 80], P(('ctx', 'exp'))
- grad_dt_proj: float32 [48, 1536], P(None, ('ctx', 'exp'))
- grad_dt_bias: float32 [1536], P(('ctx', 'exp'))
- grad_log_decay: float32 [1536, 16], P(('ctx', 'exp'))
- grad_skip_gain: float32 [1536], P(('ctx', 'exp'))
- grad_out_proj: float32 [1536, 768], P(('ctx', 'exp'))
- grad_moe_gain: float32 [768], P(('ctx', 'exp'))
- grad_router: float32 [768, 8], P(('ctx', 'exp'))
- grad_expert_in: float32 [8, 768, 3072], P('exp', None, 'ctx')
- grad_expert_out: float32 [8, 3072, 768], P('exp', 'ctx')
Inputs may be any that keep to these rules, and one draw needn't show every extreme that they name: `segments`: segment numbers start at 0 and never fall along a sequence; each sequence holds one document that begins among its first 192 positions and ends within its last 192 positions, and each sequence's last document is number 16 - 1. `routes`: among the tokens of one device (aligned blocks of 384 positions), no expert is named more than 60 times, and some expert exactly that many.
All inputs are finite; a program needn't handle non-finite values.
Results may differ from a plain program's by a relative error of at most 0.017.
Values may be sent and summed in bfloat16 or wider, within the bound.
A program may use at most 192 MiB of HBM per device.

v0:
```python
import jax
import jax.numpy as jnp
from jax import lax
from jax.sharding import PartitionSpec as P

D = 768
DI = 1536
NS = 16
R = 48
KC = 4
STATE_BLOCK = 32


EPS = 1e-05


def shifted(value, axis, steps):
    count = lax.axis_size(axis)
    initial, last = (max(0, -steps), min(count, count - steps))
    return lax.ppermute(value, axis, [(source, source + steps) for source in range(initial, last)])


def rms_scale(values, gain):
    return values * lax.rsqrt(jnp.mean(values * values, axis=-1, keepdims=True) + EPS) * gain


def conv_local(ext_rows, taps, bias, ext_ids):
    length = ext_rows.shape[0] - (KC - 1)
    own_ids = ext_ids[KC - 1 :]
    result = jnp.zeros((length, ext_rows.shape[1]), jnp.float32) + bias[None, :]
    for offset in range(KC):
        same_doc = (ext_ids[offset : offset + length] == own_ids).astype(jnp.float32)
        result = (
            result
            + taps[:, offset][None, :] * ext_rows[offset : offset + length] * same_doc[:, None]
        )
    return result


def forward_block(state_in, block_in, a_swap):
    step_rows, b_rows, c_rows, xs_rows, keep_rows = block_in
    decays = jnp.exp(step_rows[:, None, :] * a_swap[None]) * keep_rows[:, None, None]
    pushes = b_rows[:, :, None] * (step_rows * xs_rows)[:, None, :]
    states = []
    state_now = state_in
    for position in range(step_rows.shape[0]):
        state_now = decays[position] * state_now + pushes[position]
        states.append(state_now)
    return (state_now, jnp.stack(states), decays)


def body(
    inputs,
    segments,
    routes,
    cotangent,
    norm_gain,
    in_proj,
    conv_taps,
    conv_bias,
    x_proj,
    dt_proj,
    dt_bias,
    log_decay,
    skip_gain,
    out_proj,
    moe_gain,
    router,
    expert_in,
    expert_out,
):
    (
        full_norm,
        full_in,
        full_taps,
        full_bias,
        full_xproj,
        full_dt,
        full_dtbias,
        full_decay,
        full_skip,
        full_out,
        full_moe,
        full_router,
    ) = (
        lax.all_gather(norm_gain, ("ctx", "exp"), axis=0, tiled=True),
        lax.all_gather(in_proj, ("ctx", "exp"), axis=0, tiled=True),
        lax.all_gather(conv_taps, ("ctx", "exp"), axis=0, tiled=True),
        lax.all_gather(conv_bias, ("ctx", "exp"), axis=0, tiled=True),
        lax.all_gather(x_proj, ("ctx", "exp"), axis=0, tiled=True),
        lax.all_gather(dt_proj, ("ctx", "exp"), axis=1, tiled=True),
        lax.all_gather(dt_bias, ("ctx", "exp"), axis=0, tiled=True),
        lax.all_gather(log_decay, ("ctx", "exp"), axis=0, tiled=True),
        lax.all_gather(skip_gain, ("ctx", "exp"), axis=0, tiled=True),
        lax.all_gather(out_proj, ("ctx", "exp"), axis=0, tiled=True),
        lax.all_gather(moe_gain, ("ctx", "exp"), axis=0, tiled=True),
        lax.all_gather(router, ("ctx", "exp"), axis=0, tiled=True),
    )
    tokens_here = inputs.shape[1]
    experts = router.shape[1]
    capacity = 5 * tokens_here // (4 * experts)
    flat_in = inputs[0].astype(jnp.float32)
    seg_row = segments[0]
    position = lax.axis_index("ctx")
    norm_one_value, norm_one_pull = jax.vjp(rms_scale, flat_in, full_norm.astype(jnp.float32))
    normed_one = norm_one_value.astype(jnp.bfloat16)
    mixed_in = jnp.dot(normed_one, full_in, preferred_element_type=jnp.float32)
    conv_in = mixed_in[:, :DI].astype(jnp.bfloat16)
    gate_z = mixed_in[:, DI:]
    edge_rows, edge_ids = shifted(
        (conv_in[tokens_here - (KC - 1) :], seg_row[tokens_here - (KC - 1) :].astype(jnp.bfloat16)),
        "ctx",
        1,
    )
    prior_ids = jnp.where(position > 0, edge_ids.astype(jnp.int32), -1)
    ext_ids = jnp.concatenate([prior_ids, seg_row])
    ext_rows = jnp.concatenate([edge_rows, conv_in], axis=0).astype(jnp.float32)
    conv_out, conv_pull = jax.vjp(
        lambda rows_in, taps_in, bias_in: conv_local(rows_in, taps_in, bias_in, ext_ids),
        ext_rows,
        full_taps.astype(jnp.float32),
        full_bias.astype(jnp.float32),
    )
    silu_value, silu_pull = jax.vjp(jax.nn.silu, conv_out)
    xs_val = silu_value.astype(jnp.bfloat16)
    xs_wide = xs_val.astype(jnp.float32)
    projected = jnp.dot(xs_val, full_xproj, preferred_element_type=jnp.float32)
    delta_low = projected[:, :R].astype(jnp.bfloat16)
    b_rows = projected[:, R : R + NS]
    c_rows = projected[:, R + NS :]
    dt_pre = jnp.dot(delta_low, full_dt, preferred_element_type=jnp.float32) + full_dtbias.astype(
        jnp.float32
    )
    step_size = jax.nn.softplus(dt_pre)
    a_swap = -jnp.exp(full_decay.astype(jnp.float32)).T
    earlier = jnp.concatenate([prior_ids[KC - 2 :], seg_row[:-1]])
    keep_mask = (earlier == seg_row).astype(jnp.float32)
    block_count = tokens_here // STATE_BLOCK

    def split_rows(values):
        return values.reshape((block_count, STATE_BLOCK) + values.shape[1:])

    forward_inputs = (
        split_rows(step_size),
        split_rows(b_rows),
        split_rows(c_rows),
        split_rows(xs_wide),
        split_rows(keep_mask),
    )

    def summary_pass(carried, block_in):
        state_end, stacked, decays = forward_block(carried[0], block_in, a_swap)
        return ((state_end, carried[1] * jnp.prod(decays, axis=0)), None)

    zeros_state = jnp.zeros((NS, DI), jnp.float32)
    ones_state = jnp.ones((NS, DI), jnp.float32)
    (block_end, block_product), unused = lax.scan(
        summary_pass, (zeros_state, ones_state), forward_inputs
    )
    all_products, all_ends = (
        lax.all_gather(block_product[None].astype(jnp.bfloat16), "ctx", axis=0, tiled=True).astype(
            jnp.float32
        ),
        lax.all_gather(block_end[None].astype(jnp.bfloat16), "ctx", axis=0, tiled=True).astype(
            jnp.float32
        ),
    )

    def fold_start(index_now, start_now):
        return jnp.where(
            index_now < position,
            all_products[index_now] * start_now + all_ends[index_now],
            start_now,
        )

    start_state = lax.fori_loop(0, all_products.shape[0], fold_start, zeros_state)

    def output_pass(state_now, block_in):
        state_end, stacked, decays = forward_block(state_now, block_in, a_swap)
        return (state_end, (jnp.sum(stacked * block_in[2][:, :, None], axis=1), state_now))

    unused_end, (scan_rows, block_starts) = lax.scan(output_pass, start_state, forward_inputs)
    skip_wide = full_skip.astype(jnp.float32)
    scanned_y = scan_rows.reshape(tokens_here, DI) + skip_wide * xs_wide
    gated_wide, gated_pull = jax.vjp(
        lambda scan_in, gate_in: scan_in * jax.nn.silu(gate_in), scanned_y, gate_z
    )
    gated = gated_wide.astype(jnp.bfloat16)
    mixed = jnp.dot(gated, full_out, preferred_element_type=jnp.float32)
    residual = flat_in + mixed
    norm_two_value, norm_two_pull = jax.vjp(rms_scale, residual, full_moe.astype(jnp.float32))
    normed_two = norm_two_value.astype(jnp.bfloat16)
    logits = jnp.dot(normed_two, full_router, preferred_element_type=jnp.float32)
    probability = jax.nn.softmax(logits, axis=-1)
    route_ids = routes[0, :, 0]
    one_hot = route_ids[:, None] == jnp.arange(experts, dtype=jnp.int32)[None, :]
    one_float = one_hot.astype(jnp.float32)
    gate_val = jnp.sum(probability * one_float, axis=1)
    running = jnp.cumsum(one_hot.astype(jnp.int32), axis=0)
    slot_index = jnp.sum(running * one_hot.astype(jnp.int32), axis=1) - 1
    target = route_ids * capacity + slot_index
    buffer = (
        jnp.zeros((experts * capacity, D), jnp.bfloat16)
        .at[target]
        .set(normed_two)
        .reshape(experts, capacity, D)
    )
    full_expert_in, full_expert_out = (
        lax.all_gather(expert_in, "ctx", axis=2, tiled=True),
        lax.all_gather(expert_out, "ctx", axis=1, tiled=True),
    )
    weight_in = full_expert_in[0]
    weight_out = full_expert_out[0]
    rows_in = lax.all_to_all(buffer, "exp", split_axis=0, concat_axis=0, tiled=True)
    hidden_pre = jnp.einsum("srd,df->srf", rows_in, weight_in, preferred_element_type=jnp.float32)
    active = jax.nn.gelu(hidden_pre, approximate=False).astype(jnp.bfloat16)
    result = jnp.einsum(
        "srf,fd->srd", active, weight_out, preferred_element_type=jnp.float32
    ).astype(jnp.bfloat16)
    expert_result, hidden_pre, active, received = (result, hidden_pre, active, rows_in)
    returned = lax.all_to_all(expert_result, "exp", split_axis=0, concat_axis=0, tiled=True)
    picked = returned.reshape(-1, D)[target].astype(jnp.float32)
    outcome = residual + gate_val[:, None] * picked
    out_block = outcome.astype(jnp.bfloat16)[None]
    grad_out = cotangent[0].astype(jnp.float32)
    grad_gate = jnp.sum(grad_out * picked, axis=1)
    grad_pick = (grad_out * gate_val[:, None]).astype(jnp.bfloat16)
    grad_buffer = (
        jnp.zeros((experts * capacity, D), jnp.bfloat16)
        .at[target]
        .set(grad_pick)
        .reshape(experts, capacity, D)
    )
    grad_result = lax.all_to_all(grad_buffer, "exp", split_axis=0, concat_axis=0, tiled=True)
    grad_active = jnp.einsum(
        "srd,fd->srf", grad_result, weight_out, preferred_element_type=jnp.float32
    )
    grad_expert_out = jnp.einsum(
        "srf,srd->fd", active, grad_result, preferred_element_type=jnp.float32
    )
    gelu_value, gelu_pull = jax.vjp(
        lambda values: jax.nn.gelu(values, approximate=False), hidden_pre
    )
    grad_hidden = gelu_pull(grad_active)[0].astype(jnp.bfloat16)
    grad_expert_in = jnp.einsum(
        "srd,srf->df", received, grad_hidden, preferred_element_type=jnp.float32
    )
    grad_rows = jnp.einsum(
        "srf,df->srd", grad_hidden, weight_in, preferred_element_type=jnp.float32
    ).astype(jnp.bfloat16)
    grad_sent = lax.all_to_all(grad_rows, "exp", split_axis=0, concat_axis=0, tiled=True)
    grad_from_experts = grad_sent.reshape(-1, D)[target].astype(jnp.float32)
    grad_w_in, grad_w_out = (
        lax.psum_scatter(
            grad_expert_in[None].astype(jnp.bfloat16), "ctx", scatter_dimension=2, tiled=True
        ).astype(jnp.float32),
        lax.psum_scatter(
            grad_expert_out[None].astype(jnp.bfloat16), "ctx", scatter_dimension=1, tiled=True
        ).astype(jnp.float32),
    )
    grad_probs = grad_gate[:, None] * one_float
    grad_logits = (
        probability * (grad_probs - jnp.sum(grad_probs * probability, axis=1, keepdims=True))
    ).astype(jnp.bfloat16)
    grad_router = jnp.dot(normed_two.T, grad_logits, preferred_element_type=jnp.float32)
    grad_normed_two = grad_from_experts + jnp.dot(
        grad_logits, full_router.T, preferred_element_type=jnp.float32
    )
    grad_resid_norm, grad_moe_gain = norm_two_pull(grad_normed_two)
    grad_resid = grad_out + grad_resid_norm
    grad_mixed = grad_resid.astype(jnp.bfloat16)
    grad_gated = jnp.dot(grad_mixed, full_out.T, preferred_element_type=jnp.float32)
    grad_out_proj = jnp.dot(gated.T, grad_mixed, preferred_element_type=jnp.float32)
    grad_y, grad_z = gated_pull(grad_gated)
    grad_skip = jnp.sum(grad_y * xs_wide, axis=0)
    grad_y_rows = split_rows(grad_y)

    def zero_adjoint(inflow, block_in):
        step_rows, b_part, c_part, xs_rows, keep_rows, grad_part = block_in
        decays = jnp.exp(step_rows[:, None, :] * a_swap[None]) * keep_rows[:, None, None]
        for place in reversed(range(step_rows.shape[0])):
            adjoint = c_part[place][:, None] * grad_part[place][None, :] + inflow
            inflow = decays[place] * adjoint
        return (inflow, None)

    local_inflow, unused_zero = lax.scan(
        zero_adjoint, zeros_state, forward_inputs + (grad_y_rows,), reverse=True
    )
    all_inflows = lax.all_gather(
        local_inflow[None].astype(jnp.bfloat16), "ctx", axis=0, tiled=True
    ).astype(jnp.float32)
    total_ctx = all_inflows.shape[0]

    def fold_end(step_index, end_now):
        source = total_ctx - 1 - step_index
        return jnp.where(
            source > position, all_inflows[source] + all_products[source] * end_now, end_now
        )

    end_inflow = lax.fori_loop(0, total_ctx, fold_end, zeros_state)

    def full_adjoint(inflow, block_in):
        step_rows, b_part, c_part, xs_rows, keep_rows, grad_part, start_in = block_in
        state_end, stacked, decays = forward_block(
            start_in, (step_rows, b_part, c_part, xs_rows, keep_rows), a_swap
        )
        previous = jnp.concatenate([start_in[None], stacked[:-1]], axis=0)
        adjoints = []
        for place in reversed(range(step_rows.shape[0])):
            adjoint = c_part[place][:, None] * grad_part[place][None, :] + inflow
            inflow = decays[place] * adjoint
            adjoints.append(adjoint)
        adjoint_stack = jnp.stack(adjoints[::-1])
        decay_grad = adjoint_stack * previous * decays
        along_b = jnp.sum(adjoint_stack * b_part[:, :, None], axis=1)
        grad_step = along_b * xs_rows + jnp.sum(decay_grad * a_swap[None], axis=1)
        grad_b = jnp.sum(adjoint_stack * (step_rows * xs_rows)[:, None, :], axis=2)
        grad_xs = along_b * step_rows
        grad_c = jnp.sum(stacked * grad_part[:, None, :], axis=2)
        grad_a = jnp.sum(decay_grad * step_rows[:, None, :], axis=0)
        return (inflow, (grad_step, grad_b, grad_xs, grad_c, grad_a))

    unused_in, (grad_steps, grad_bs, grad_xss, grad_cs, grad_as) = lax.scan(
        full_adjoint, end_inflow, forward_inputs + (grad_y_rows, block_starts), reverse=True
    )
    grad_step_all = grad_steps.reshape(tokens_here, DI)
    grad_log_decay = (jnp.sum(grad_as, axis=0) * a_swap).T
    soft_slope = jax.nn.sigmoid(dt_pre)
    grad_pre_wide = grad_step_all * soft_slope
    grad_dt_bias = jnp.sum(grad_pre_wide, axis=0)
    grad_dt_pre = grad_pre_wide.astype(jnp.bfloat16)
    grad_dt_proj = jnp.dot(delta_low.T, grad_dt_pre, preferred_element_type=jnp.float32)
    grad_delta = jnp.dot(grad_dt_pre, full_dt.T, preferred_element_type=jnp.float32)
    grad_projected = jnp.concatenate(
        [grad_delta, grad_bs.reshape(tokens_here, NS), grad_cs.reshape(tokens_here, NS)], axis=1
    ).astype(jnp.bfloat16)
    grad_x_proj = jnp.dot(xs_val.T, grad_projected, preferred_element_type=jnp.float32)
    grad_xs_total = (
        skip_wide * grad_y
        + grad_xss.reshape(tokens_here, DI)
        + jnp.dot(grad_projected, full_xproj.T, preferred_element_type=jnp.float32)
    )
    grad_conv = silu_pull(grad_xs_total)[0]
    grad_ext, grad_taps, grad_cbias = conv_pull(grad_conv)
    from_next = shifted(grad_ext[: KC - 1], "ctx", -1)
    grad_conv_in = grad_ext[KC - 1 :] + jnp.concatenate(
        [jnp.zeros((tokens_here - (KC - 1), DI), jnp.float32), from_next], axis=0
    )
    grad_mixed_in = jnp.concatenate([grad_conv_in, grad_z], axis=1).astype(jnp.bfloat16)
    grad_in_proj = jnp.dot(normed_one.T, grad_mixed_in, preferred_element_type=jnp.float32)
    grad_normed_one = jnp.dot(grad_mixed_in, full_in.T, preferred_element_type=jnp.float32)
    grad_inputs_norm, grad_norm_gain = norm_one_pull(grad_normed_one)
    grad_inputs = grad_resid + grad_inputs_norm
    shares = (
        lax.psum_scatter(grad_norm_gain, ("ctx", "exp"), scatter_dimension=0, tiled=True),
        lax.psum_scatter(grad_in_proj, ("ctx", "exp"), scatter_dimension=0, tiled=True),
        lax.psum_scatter(grad_taps, ("ctx", "exp"), scatter_dimension=0, tiled=True),
        lax.psum_scatter(grad_cbias, ("ctx", "exp"), scatter_dimension=0, tiled=True),
        lax.psum_scatter(grad_x_proj, ("ctx", "exp"), scatter_dimension=0, tiled=True),
        lax.psum_scatter(grad_dt_proj, ("ctx", "exp"), scatter_dimension=1, tiled=True),
        lax.psum_scatter(grad_dt_bias, ("ctx", "exp"), scatter_dimension=0, tiled=True),
        lax.psum_scatter(grad_log_decay, ("ctx", "exp"), scatter_dimension=0, tiled=True),
        lax.psum_scatter(grad_skip, ("ctx", "exp"), scatter_dimension=0, tiled=True),
        lax.psum_scatter(grad_out_proj, ("ctx", "exp"), scatter_dimension=0, tiled=True),
        lax.psum_scatter(grad_moe_gain, ("ctx", "exp"), scatter_dimension=0, tiled=True),
        lax.psum_scatter(grad_router, ("ctx", "exp"), scatter_dimension=0, tiled=True),
    )
    return (
        out_block,
        grad_inputs[None],
        shares[0],
        shares[1],
        shares[2],
        shares[3],
        shares[4],
        shares[5],
        shares[6],
        shares[7],
        shares[8],
        shares[9],
        shares[10],
        shares[11],
        grad_w_in,
        grad_w_out,
    )


def solution(mesh):
    placed = (
        P("exp", "ctx", None),
        P("exp", "ctx"),
        P("exp", "ctx", None),
        P("exp", "ctx", None),
        P(("ctx", "exp")),
        P(("ctx", "exp"), None),
        P(("ctx", "exp"), None),
        P(("ctx", "exp")),
        P(("ctx", "exp"), None),
        P(None, ("ctx", "exp")),
        P(("ctx", "exp")),
        P(("ctx", "exp"), None),
        P(("ctx", "exp")),
        P(("ctx", "exp"), None),
        P(("ctx", "exp")),
        P(("ctx", "exp"), None),
        P("exp", None, "ctx"),
        P("exp", "ctx", None),
    )
    return jax.shard_map(
        body,
        mesh=mesh,
        in_specs=placed,
        out_specs=(
            P("exp", "ctx", None),
            P("exp", "ctx", None),
            P(("ctx", "exp")),
            P(("ctx", "exp"), None),
            P(("ctx", "exp"), None),
            P(("ctx", "exp")),
            P(("ctx", "exp"), None),
            P(None, ("ctx", "exp")),
            P(("ctx", "exp")),
            P(("ctx", "exp"), None),
            P(("ctx", "exp")),
            P(("ctx", "exp"), None),
            P(("ctx", "exp")),
            P(("ctx", "exp"), None),
            P("exp", None, "ctx"),
            P("exp", "ctx", None),
        ),
        check_vma=False,
    )
```

profile of v0, /device:TPU:0, one launch (start us, length us, event | category | flops | bytes accessed | tf_op | source)
XLA Modules:
  0.0 3055.2 jit_solution(12441787584396348243)
XLA Ops:
  18.3 42.2 %all-reduce.21 = (bf16[768]{0:T(1024)(128)(2,1)S(1)}, bf16[1536]{0:T(1024)(128)(2,1)S(1)}, bf16[1536]{0:T(1024)(128)(2,1)S(1)}, bf16[1536]{0:T(1024)(128)(2,1)S(1)}, bf16[768]{0:T(1024)(128)(2,1)S(1)}) all-reduce(bf16[768]{0:T(1024)(128)(2,1)S(1)} %dynamic-update-slice.1, ...), channel_id=1, replica_groups=mesh['ctx'=4,'exp'=8] {'ctx','exp'}, use_global_device_ids=true, to_apply=%add.10 | all-reduce | flops 6144 | bytes 24576
  61.8 66.0 %all-gather.3 = bf16[32,48,4]{1,2,0:T(4,128)(2,1)S(1)} all-gather(bf16[1,48,4]{1,2,0:T(4,128)(2,1)S(1)} %bitcast.2310), channel_id=1, replica_groups=mesh['ctx'=4,'exp'=8] {'ctx','exp'}, dimensions={0}, use_global_device_ids=true | all-gather | bytes 12672 | tf_op jit(solution)/shard_map/all_gather | solution.py:88
  128.0 66.6 %all_gather.55 = bf16[1536,80]{1,0:T(8,128)(2,1)S(1)} all-gather(bf16[48,80]{1,0:T(8,128)(2,1)S(1)} %copy-done.98), channel_id=1, replica_groups=mesh['ctx'=4,'exp'=8] {'ctx','exp'}, dimensions={0}, use_global_device_ids=true | all-gather | bytes 253440 | tf_op jit(solution)/shard_map/all_gather | solution.py:90
  194.7 68.3 %all_gather.56 = bf16[48,1536]{0,1:T(8,128)(2,1)S(1)} all-gather(bf16[48,48]{0,1:T(8,128)(2,1)S(1)} %copy.78), channel_id=1, replica_groups=mesh['ctx'=4,'exp'=8] {'ctx','exp'}, dimensions={1}, use_global_device_ids=true | all-gather | bytes 152064 | tf_op jit(solution)/shard_map/all_gather | solution.py:91
  263.1 64.0 %all-gather.4 = bf16[32,48,16]{1,2,0:T(8,128)(2,1)S(1)} all-gather(bf16[1,48,16]{1,2,0:T(8,128)(2,1)S(1)} %bitcast.2308), channel_id=1, replica_groups=mesh['ctx'=4,'exp'=8] {'ctx','exp'}, dimensions={0}, use_global_device_ids=true | all-gather | bytes 50688 | tf_op jit(solution)/shard_map/all_gather | solution.py:93
  331.4 6.6 fusion.483
  351.1 100.5 %while.98 = (s32[]{:T(128)}, f32[16,1536]{1,0:T(8,128)}, f32[16,1536]{1,0:T(8,128)S(1)}, f32[12,32,1536]{2,1,0:T(8,128)}, f32[16,1536]{1,0:T(8,128)S(1)}, /*inde...) while((s32[]{:T(128)}, f32[16,1536]{1,0:T(8,128)}, ...), condition=%wide.region_3.4_spmd.clone, body=%wide.region_1.3_spmd.clone.sunk | while | flops 4816899 | bytes 14653952 | solution.py:157
  451.6 8.5 all-gather
  461.1 5.8 all-gather.1
  470.8 474.5 %while.96 = (s32[]{:T(128)}, f32[16,1536]{1,0:T(8,128)S(1)}, f32[12,32,1536]{2,1,0:T(8,128)}, f32[12,16,1536]{2,1,0:T(8,128)}, f32[12,32,1536]{2,1,0:T(8,128)}, ...) while((s32[]{:T(128)}, f32[16,1536]{1,0:T(8,128)S(1)}, ...), condition=%wide.region_8.9_spmd, body=%wide.region_6.8_spmd.sunk | while | flops 6291457 | bytes 54081076 | solution.py:182
  960.3 20.8 all-to-all-done
  981.1 6.1 fusion.385
  989.8 15.1 multiply_convert_fusion
  1004.9 6.8 fusion.393
  1015.9 75.5 %all-gather.5 = bf16[32,24,8]{1,2,0:T(8,128)(2,1)S(1)} all-gather(bf16[1,24,8]{1,2,0:T(8,128)(2,1)S(1)} %bitcast.2309), channel_id=1, replica_groups=mesh['ctx'=4,'exp'=8] {'ctx','exp'}, dimensions={0}, use_global_device_ids=true | all-gather | bytes 12672 | tf_op jit(solution)/shard_map/all_gather | solution.py:97
  1103.3 21.9 all_to_all.20
  1125.3 8.6 add_convert_fusion
  1143.4 19.2 all-to-all-done.3
  1171.9 6.2 multiply_reduce_fusion.6
  1178.1 141.7 %while.100 = (s32[]{:T(128)}, f32[16,1536]{1,0:T(8,128)S(1)}, f32[12,32,1536]{2,1,0:T(8,128)}, f32[16,1536]{1,0:T(8,128)S(1)}, f32[12,32]{1,0:T(8,128)}, /*index...) while((s32[]{:T(128)}, f32[16,1536]{1,0:T(8,128)S(1)}, ...), condition=%wide.region_22.23_spmd.clone, body=%wide.region_21.22_spmd.clone.sunk | while | flops 3956771 | bytes 7773559 | solution.py:286
  1319.8 5.8 all-gather.2
  1335.6 949.3 %while.97 = (s32[]{:T(128)}, f32[16,1536]{1,0:T(8,128)S(1)}, f32[12,32,1536]{2,1,0:T(8,128)}, bf16[12,32,16]{2,1,0:T(8,128)(2,1)}, f32[12,32,1536]{2,1,0:T(8,128...) while((s32[]{:T(128)}, f32[16,1536]{1,0:T(8,128)S(1)}, ...), condition=%wide.region_31.32_spmd, body=%wide.region_25.31_spmd.sunk | while | flops 18652192 | bytes 93043200 | solution.py:323
  1403.7 4.8 multiply_reduce_fusion.18
  1483.1 4.8 multiply_reduce_fusion.18
  1562.1 4.8 multiply_reduce_fusion.18
  1641.2 4.8 multiply_reduce_fusion.18
  1720.4 4.8 multiply_reduce_fusion.18
  1799.3 4.8 multiply_reduce_fusion.18
  1878.3 4.8 multiply_reduce_fusion.18
  1957.4 4.8 multiply_reduce_fusion.18
  2036.6 4.8 multiply_reduce_fusion.18
  2115.6 4.8 multiply_reduce_fusion.18
  2274.0 4.8 multiply_reduce_fusion.18
  2292.6 5.7 multiply_reduce_fusion.10
  2302.9 6.7 fusion.374
  2310.7 6.2 fusion.373
  2319.7 4.9 fusion.416
  2331.7 5.4 fusion.386
  2338.3 5.3 fusion.397
  2343.7 38.9 %all-reduce.20 = (f32[768]{0:T(1024)S(1)}, f32[1536]{0:T(1024)S(1)}, f32[1536]{0:T(1024)S(1)}, f32[1536]{0:T(1024)S(1)}, f32[768]{0:T(1024)S(1)}, /*index=5*/f32[768,8]{0,1:T(8,128)S(1)}) all-reduce(f32[768]{0:T(1024)S(1)} %get-tuple-element.1152, ...), channel_id=5, replica_groups=mesh['ctx'=4,'exp'=8] {'ctx','exp'}, use_global_device_ids=true, to_apply=%region_34.35.clone | all-reduce | flops 12288 | bytes 98304
  2387.6 5.8 reduce-scatter.26.cloned.1.call-done
  2394.7 98.2 %reduce-scatter.30.cloned.1.call-done = f32[48,16]{1,0:T(8,128)} async-done(((f32[1536,16]{1,0:T(8,128)}), f32[48,16]{1,0:T(8,128)}) %reduce-scatter.30.cloned.1.call-update) | async-done | bytes 3088
  2494.3 98.2 %reduce-scatter.28.cloned.1.call-done = f32[48,48]{1,0:T(8,128)} async-done(((f32[1536,48]{1,0:T(8,128)}), f32[48,48]{1,0:T(8,128)}) %reduce-scatter.28.cloned.1.call-update) | async-done | bytes 9232
  2594.0 48.1 %reduce-scatter.24.cloned.1.call-done = bf16[1,768,768]{2,1,0:T(8,128)(2,1)} async-done(((bf16[1,3072,768]{2,1,0:T(8,128)(2,1)}), bf16[1,768,768]{2,1,0:T(8,128)(2,1)}) %reduce-scatter.24.cloned.1.call-update) | async-done | bytes 1179664 | tf_op jit(solution)/shard_map/reduce_scatter | solution.py:257
  2644.9 47.7 %reduce-scatter.22.cloned.1.call-done = bf16[1,768,768]{2,1,0:T(8,128)(2,1)} async-done(((bf16[1,768,3072]{2,1,0:T(8,128)(2,1)}), bf16[1,768,768]{2,1,0:T(8,128)(2,1)}) %reduce-scatter.22.cloned.1.call-update) | async-done | bytes 1179664 | tf_op jit(solution)/shard_map/reduce_scatter | solution.py:254
  2695.5 98.2 %reduce-scatter.18.cloned.1.call-done = f32[48,80]{1,0:T(8,128)} async-done(((f32[1536,80]{1,0:T(8,128)}), f32[48,80]{1,0:T(8,128)}) %reduce-scatter.18.cloned.1.call-update) | async-done | bytes 15376 | tf_op jit(solution)/shard_map/reduce_scatter | solution.py:359
  2793.7 112.1 %reduce-scatter.20.cloned.1.call-done = f32[48,768]{1,0:T(8,128)} async-done(((f32[1536,768]{1,0:T(8,128)}), f32[48,768]{1,0:T(8,128)}) %reduce-scatter.20.cloned.1.call-update) | async-done | bytes 147472 | tf_op jit(solution)/shard_map/reduce_scatter | solution.py:364
  2905.8 142.1 %reduce-scatter.16.cloned.1.call-done = f32[24,3072]{1,0:T(8,128)} async-done(((f32[768,3072]{1,0:T(8,128)}), f32[24,3072]{1,0:T(8,128)}) %reduce-scatter.16.cloned.1.call-update) | async-done | bytes 294928 | tf_op jit(solution)/shard_map/reduce_scatter | solution.py:356
  (2531 shorter events, 1744.6 us)
Async XLA Ops:
  7.2 324.2 %copy-start.24 = (bf16[1,384,768]{2,1,0:T(8,128)(2,1)S(1)}, bf16[1,384,768]{2,1,0:T(8,128)(2,1)}, u32[]{:S(2)}) copy-start(bf16[1,384,768]{2,1,0:T(8,128)(2,1)} %param.30) | copy-start | bytes 1769476
  7.2 54.6 %copy-start.111 = (bf16[48,4]{0,1:T(4,128)(2,1)S(1)}, bf16[48,4]{0,1:T(4,128)(2,1)}, u32[]{:S(2)}) copy-start(bf16[48,4]{0,1:T(4,128)(2,1)} %param.36) | copy-start | bytes 1156
  7.2 120.8 %copy-start.98 = (bf16[48,80]{1,0:T(8,128)(2,1)S(1)}, bf16[48,80]{1,0:T(8,128)(2,1)}, u32[]{:S(2)}) copy-start(bf16[48,80]{1,0:T(8,128)(2,1)} %param.38) | copy-start | bytes 23044
  7.2 187.4 %copy-start.99 = (bf16[48,48]{1,0:T(8,128)(2,1)S(1)}, bf16[48,48]{1,0:T(8,128)(2,1)}, u32[]{:S(2)}) copy-start(bf16[48,48]{1,0:T(8,128)(2,1)} %param.39) | copy-start | bytes 13828
  7.2 255.9 %copy-start.109 = (bf16[48,16]{0,1:T(8,128)(2,1)S(1)}, bf16[48,16]{0,1:T(8,128)(2,1)}, u32[]{:S(2)}) copy-start(bf16[48,16]{0,1:T(8,128)(2,1)} %param.41) | copy-start | bytes 4612
  7.2 320.2 %copy-start.108 = (s32[1,384,1]{1,2,0:T(1,128)S(1)}, s32[1,384,1]{1,2,0:T(1,128)}, u32[]{:S(2)}) copy-start(s32[1,384,1]{1,2,0:T(1,128)} %param.32) | copy-start | bytes 4612
  7.2 324.1 %all-gather.11.cloned.1.call-start = ((), (), s32[]{:S(2)}) async-start(), calls=%async_computation.12 | async-start | bytes 4866048 | tf_op jit(solution)/shard_map/all_gather | solution.py:87
  8.0 941.6 %all-gather.13.cloned.1.call-start = ((), (), s32[]{:S(2)}) async-start(), calls=%async_computation.13 | async-start | bytes 2433024 | tf_op jit(solution)/shard_map/all_gather | solution.py:95
  8.7 951.5 %all-gather.15.cloned.1.call-start = ((), (), s32[]{:S(2)}) async-start(), calls=%async_computation.14 | async-start | bytes 5898240 | tf_op jit(solution)/shard_map/all_gather | solution.py:209
  9.5 995.5 %all-gather.17.cloned.1.call-start = ((), (), s32[]{:S(2)}) async-start(), calls=%async_computation.15 | async-start | bytes 5898240 | tf_op jit(solution)/shard_map/all_gather | solution.py:210
  10.2 319.1 %collective-permute-start.1 = (bf16[3]{0:T(256)(128)(2,1)S(1)}, bf16[3]{0:T(256)(128)(2,1)S(1)}, u32[]{:S(2)}, u32[]{:S(2)}) collective-permute-start(bf16[3]{0:T(256)(128)(2,1)S(1)} %fusion.438), channel_id=1, source_target_pairs={{0,8},{8,16},{16,24},{1,9},{9,17},{17,25},{2,10},{10,18},{18,26},{... | collective-permute-start | bytes 26 | tf_op jit(solution)/shard_map/ppermute | solution.py:20
  60.5 277.5 %copy-start.58 = (f32[768]{0:T(1024)}, f32[768]{0:T(1024)S(1)}, u32[]{:S(2)}) copy-start(f32[768]{0:T(1024)S(1)} %convert_element_type.164) | copy-start | bytes 9220
  61.7 132.9 %copy-start.95 = (f32[384]{0:T(512)}, f32[384]{0:T(512)S(1)}, u32[]{:S(2)}) copy-start(f32[384]{0:T(512)S(1)} %fusion.404) | copy-start | bytes 4612
  61.8 276.2 %copy-start.60 = (f32[384]{0:T(512)}, f32[384]{0:T(512)S(1)}, u32[]{:S(2)}) copy-start(f32[384]{0:T(512)S(1)} %fusion.435) | copy-start | bytes 4612
  128.0 212.4 %copy-start.85 = (f32[1536]{0:T(1024)}, f32[1536]{0:T(1024)S(1)}, u32[]{:S(2)}) copy-start(f32[1536]{0:T(1024)S(1)} %get-tuple-element.1154) | copy-start | bytes 18436
  128.0 212.4 %copy-start.87 = (f32[1536]{0:T(1024)}, f32[1536]{0:T(1024)S(1)}, u32[]{:S(2)}) copy-start(f32[1536]{0:T(1024)S(1)} %get-tuple-element.1155) | copy-start | bytes 18436
  128.0 212.4 %copy-start.89 = (f32[1536]{0:T(1024)}, f32[1536]{0:T(1024)S(1)}, u32[]{:S(2)}) copy-start(f32[1536]{0:T(1024)S(1)} %get-tuple-element.1156) | copy-start | bytes 18436
  128.0 212.4 %copy-start.91 = (f32[1536]{0:T(1024)}, f32[1536]{0:T(1024)S(1)}, u32[]{:S(2)}) copy-start(f32[1536]{0:T(1024)S(1)} %get-tuple-element.1157) | copy-start | bytes 18436
  194.6 149.1 %copy-start.43 = (bf16[1536,80]{1,0:T(8,128)(2,1)}, bf16[1536,80]{1,0:T(8,128)(2,1)S(1)}, u32[]{:S(2)}) copy-start(bf16[1536,80]{1,0:T(8,128)(2,1)S(1)} %all_gather.55) | copy-start | bytes 737284
  263.0 84.4 %copy-start.45 = (bf16[48,1536]{0,1:T(8,128)(2,1)}, bf16[48,1536]{0,1:T(8,128)(2,1)S(1)}, u32[]{:S(2)}) copy-start(bf16[48,1536]{0,1:T(8,128)(2,1)S(1)} %all_gather.56) | copy-start | bytes 442372
  327.4 842.9 %copy-start.75 = (f32[1536]{0:T(1024)}, f32[1536]{0:T(1024)S(1)}, u32[]{:S(2)}) copy-start(f32[1536]{0:T(1024)S(1)} %convert_element_type.183) | copy-start | bytes 18436
  327.5 839.1 %copy-start.73 = (s32[384]{0:T(512)}, s32[384]{0:T(512)S(1)}, u32[]{:S(2)}) copy-start(s32[384]{0:T(512)S(1)} %reduce.71) | copy-start | bytes 4612
  338.0 2.1 collective-permute-start
  470.8 474.5 %copy-start.10 = (bf16[384,1536]{1,0:T(8,128)(2,1)S(1)}, bf16[384,1536]{1,0:T(8,128)(2,1)}, u32[]{:S(2)}) copy-start(bf16[384,1536]{1,0:T(8,128)(2,1)} %copy-done.9) | copy-start | bytes 3538948
  956.3 24.8 all-to-all-start
  1011.7 81.3 %all-to-all-start.1 = ((bf16[8,60,768]{2,1,0:T(8,128)(2,1)}), bf16[8,60,768]{2,1,0:T(8,128)(2,1)}, u32[]{:S(2)}, u32[]{:S(2)}) async-start(bf16[8,60,768]{2,1,0:T(8,128)(2,1)} %fusion.393), calls=%async_computation.1 | async-start | bytes 1572864 | tf_op jit(solution)/shard_map/all_to_all | solution.py:221
  1092.9 73.6 %copy-start.56 = (f32[384,8]{0,1:T(8,128)}, f32[384,8]{0,1:T(8,128)S(1)}, u32[]{:S(2)}) copy-start(f32[384,8]{0,1:T(8,128)S(1)} %get-tuple-element.1532) | copy-start | bytes 36868
  1092.9 73.6 %copy-start.79 = (f32[384]{0:T(512)}, f32[384]{0:T(512)S(1)}, u32[]{:S(2)}) copy-start(f32[384]{0:T(512)S(1)} %get-tuple-element.1531) | copy-start | bytes 4612
  1093.0 73.6 %copy-start.83 = (f32[384]{0:T(512)}, f32[384]{0:T(512)S(1)}, u32[]{:S(2)}) copy-start(f32[384]{0:T(512)S(1)} %fusion.431) | copy-start | bytes 4612
  1098.4 68.2 %copy-start.81 = (f32[384]{0:T(512)}, f32[384]{0:T(512)S(1)}, u32[]{:S(2)}) copy-start(f32[384]{0:T(512)S(1)} %fusion.403) | copy-start | bytes 4612
  1098.4 68.2 %copy-start.93 = (f32[384]{0:T(512)}, f32[384]{0:T(512)S(1)}, u32[]{:S(2)}) copy-start(f32[384]{0:T(512)S(1)} %get-tuple-element.1158) | copy-start | bytes 4612
  1103.3 32.2 %slice-start = ((s8[4718592]{0:T(1024)(128)(4,1)}), s8[4194304]{0:T(1024)(128)(4,1)S(1)}, s32[]{:S(2)}) async-start(s8[4718592]{0:T(1024)(128)(4,1)} %bitcast.2311), calls=%async_computation.24 | async-start | bytes 8388608
  1139.1 23.5 all-to-all-start.3
  1143.4 1250.0 %reduce-scatter.26.cloned.1.call-start = ((), (), s32[]{:S(2)}) async-start(), calls=%async_computation.21 | async-start | bytes 811008
  1433.6 22.1 copy-start.1
  1671.1 21.9 copy-start.1
  1987.3 21.9 copy-start.1
  2145.5 21.9 copy-start.1
  2224.7 21.9 copy-start.1
  2299.6 193.3 %reduce-scatter.30.cloned.1.call-start = ((), (), s32[]{:S(2)}) async-start(), calls=%async_computation.23 | async-start | bytes 811008
  2301.0 291.6 %reduce-scatter.28.cloned.1.call-start = ((), (), s32[]{:S(2)}) async-start(), calls=%async_computation.22 | async-start | bytes 811008
  2302.6 339.5 %reduce-scatter.24.cloned.1.call-start = ((), (), s32[]{:S(2)}) async-start(), calls=%async_computation.20 | async-start | bytes 5898240 | tf_op jit(solution)/shard_map/reduce_scatter | solution.py:257
  2309.6 383.0 %reduce-scatter.22.cloned.1.call-start = ((), (), s32[]{:S(2)}) async-start(), calls=%async_computation.19 | async-start | bytes 5898240 | tf_op jit(solution)/shard_map/reduce_scatter | solution.py:254
  2317.0 476.7 %reduce-scatter.18.cloned.1.call-start = ((), (), s32[]{:S(2)}) async-start(), calls=%async_computation.17 | async-start | bytes 811008 | tf_op jit(solution)/shard_map/reduce_scatter | solution.py:359
  2319.7 586.1 %reduce-scatter.20.cloned.1.call-start = ((), (), s32[]{:S(2)}) async-start(), calls=%async_computation.18 | async-start | bytes 4866048 | tf_op jit(solution)/shard_map/reduce_scatter | solution.py:364
  2324.7 723.2 %reduce-scatter.16.cloned.1.call-start = ((), (), s32[]{:S(2)}) async-start(), calls=%async_computation.16 | async-start | bytes 9732096 | tf_op jit(solution)/shard_map/reduce_scatter | solution.py:356
  2325.8 4.0 collective-permute-start.2
  2338.3 47.9 %copy-start.96 = (f32[384]{0:T(512)S(1)}, f32[384]{0:T(512)}, u32[]{:S(2)}) copy-start(f32[384]{0:T(512)} %copy-done.95) | copy-start | bytes 4612
  (427 other events, 3422.3 us)
Sparse Core Ops, SparseCore 0:
  11.0 66.5 all-gather.10
  80.5 56.0 all-gather.12
  138.2 36.8 all-gather.14
  176.5 37.4 all-gather.16
  2299.7 93.5 reduce-scatter.25
  2398.3 94.5 reduce-scatter.29
  2498.0 94.5 reduce-scatter.27
  2595.1 46.9 reduce-scatter.23
  2644.7 47.8 reduce-scatter.21
  2698.1 95.4 reduce-scatter.17
  2799.7 106.0 reduce-scatter.19
  2913.1 134.7 reduce-scatter.15
where the time goes:
time: 3100 us; the launch traced here: 3060 us
  other arithmetic  1380 us (45%)
  waiting for transfers between devices  693 us (22%)
  blocking collectives  464 us (15%)
  local copies, waits for them, and re-layouts  392 us (13%)
  matrix products  85.6 us (3%)
    while x744, other arithmetic  1010 us
    unnamed x15, waiting for transfers between devices  204 us
    reduce_scatter x1, waiting for transfers between devices, body(): lax.psum_scatter(grad_in_proj, ('ctx', 'exp'), scatter_dimension=0, tiled...  142 us
    reduce_scatter x1, waiting for transfers between devices, body(): lax.psum_scatter(grad_out_proj, ('ctx', 'exp'), scatter_dimension=0, tile...  112 us
    reduce_scatter x1, waiting for transfers between devices, body(): lax.psum_scatter(grad_x_proj, ('ctx', 'exp'), scatter_dimension=0, tiled=...  98.2 us
    unnamed x2, blocking collectives  81.1 us
    all_gather x1, blocking collectives, body(): lax.all_gather(router, ('ctx', 'exp'), axis=0, tiled=True)  75.5 us
    all_gather x1, blocking collectives, body(): lax.all_gather(dt_proj, ('ctx', 'exp'), axis=1, tiled=True)  68.3 us
  transfers between devices with their start and end apart: 18, of which 11 were waited for; matrix products, arithmetic and copies ran while one was open for 22% of the time, Pallas kernels for 0%

commit v1 on v0

--- a/solution.py
+++ b/solution.py
@@ -1,6 +1,10 @@
+import functools
+
 import jax
 import jax.numpy as jnp
 from jax import lax
+from jax.experimental import pallas as pl
+from jax.experimental.pallas import tpu as pltpu
 from jax.sharding import PartitionSpec as P
 
 D = 768
@@ -8,10 +12,247 @@
 NS = 16
 R = 48
 KC = 4
-STATE_BLOCK = 32
+LANES = 128
+UNROLL = 8
+LOG2E = 1.4426950408889634
 
 
 EPS = 1e-05
+
+def tile(ref, base, lanes):
+    return ref[pl.ds(pl.multiple_of(base, UNROLL), UNROLL), lanes]
+
+def row(rows_now, place):
+    return jnp.broadcast_to(rows_now[place : place + 1], (NS, LANES))
+
+def put_row(rows_now, place, value):
+    at = lax.broadcasted_iota(jnp.int32, (UNROLL, LANES), 0)
+    value = jnp.broadcast_to(value, (UNROLL, LANES))
+    return value if rows_now is None else jnp.where(at == place, value, rows_now)
+
+def end_kernel(width, step_ref, push_ref, b_ref, rate_ref, end_ref):
+    rows, channels = step_ref.shape
+
+    @pl.when(pl.program_id(0) == 0)
+    def _():
+        end_ref[...] = jnp.zeros_like(end_ref)
+
+    for group in range(0, channels, width):
+        pieces = [slice(at, at + LANES) for at in range(group, group + width, LANES)]
+        rates = [rate_ref[:, lanes] for lanes in pieces]
+
+        def block(index, states):
+            states = list(states)
+            steps = [tile(step_ref, index * UNROLL, lanes) for lanes in pieces]
+            pushes = [tile(push_ref, index * UNROLL, lanes) for lanes in pieces]
+            for place in range(UNROLL):
+                t = index * UNROLL + place
+                b_now = b_ref[t]
+                for k, lanes in enumerate(pieces):
+                    decay = jnp.exp2(row(steps[k], place) * rates[k])
+                    states[k] = decay * states[k] + b_now * row(pushes[k], place)
+            return tuple(states)
+
+        states = lax.fori_loop(0, rows // UNROLL, block, tuple(end_ref[:, lanes] for lanes in pieces))
+        for k, lanes in enumerate(pieces):
+            end_ref[:, lanes] = states[k]
+
+def out_kernel(width, step_ref, push_ref, b_ref, c_ref, rate_ref, start_ref, y_ref, kept_ref, first_ref, state_ref):
+    rows, channels = step_ref.shape
+
+    @pl.when(pl.program_id(0) == 0)
+    def _():
+        state_ref[...] = start_ref[...]
+
+    first_ref[0] = state_ref[...].astype(first_ref.dtype)
+    for group in range(0, channels, width):
+        pieces = [slice(at, at + LANES) for at in range(group, group + width, LANES)]
+        rates = [rate_ref[:, lanes] for lanes in pieces]
+
+        def block(index, states):
+            states = list(states)
+            steps = [tile(step_ref, index * UNROLL, lanes) for lanes in pieces]
+            pushes = [tile(push_ref, index * UNROLL, lanes) for lanes in pieces]
+            outs = [None] * len(pieces)
+            for place in range(UNROLL):
+                t = index * UNROLL + place
+                b_now = b_ref[t]
+                c_now = c_ref[t]
+                for k, lanes in enumerate(pieces):
+                    decay = jnp.exp2(row(steps[k], place) * rates[k])
+                    states[k] = decay * states[k] + b_now * row(pushes[k], place)
+                    kept_ref[t, :, lanes] = states[k].astype(kept_ref.dtype)
+                    outs[k] = put_row(outs[k], place, jnp.sum(states[k] * c_now, axis=0, keepdims=True))
+            for k, lanes in enumerate(pieces):
+                y_ref[pl.ds(pl.multiple_of(index * UNROLL, UNROLL), UNROLL), lanes] = outs[k]
+            return tuple(states)
+
+        states = lax.fori_loop(0, rows // UNROLL, block, tuple(state_ref[:, lanes] for lanes in pieces))
+        for k, lanes in enumerate(pieces):
+            state_ref[:, lanes] = states[k]
+
+def inflow_kernel(width, step_ref, grad_ref, c_ref, rate_ref, end_ref):
+    rows, channels = step_ref.shape
+
+    @pl.when(pl.program_id(0) == 0)
+    def _():
+        end_ref[...] = jnp.zeros_like(end_ref)
+
+    for group in range(0, channels, width):
+        pieces = [slice(at, at + LANES) for at in range(group, group + width, LANES)]
+        rates = [rate_ref[:, lanes] for lanes in pieces]
+
+        def block(index, flows):
+            flows = list(flows)
+            base = rows - UNROLL - index * UNROLL
+            steps = [tile(step_ref, base, lanes) for lanes in pieces]
+            grads = [tile(grad_ref, base, lanes) for lanes in pieces]
+            for place in reversed(range(UNROLL)):
+                c_now = c_ref[base + place]
+                for k, lanes in enumerate(pieces):
+                    decay = jnp.exp2(row(steps[k], place) * rates[k])
+                    flows[k] = decay * (c_now * row(grads[k], place) + flows[k])
+            return tuple(flows)
+
+        flows = lax.fori_loop(0, rows // UNROLL, block, tuple(end_ref[:, lanes] for lanes in pieces))
+        for k, lanes in enumerate(pieces):
+            end_ref[:, lanes] = flows[k]
+
+def adjoint_kernel(width, step_ref, push_ref, grad_ref, b_ref, c_ref, kept_ref, first_ref, rate_ref, end_ref,
+                   along_ref, slope_ref, gb_ref, gc_ref, ga_ref, flow_ref):
+    rows, channels = step_ref.shape
+
+    @pl.when(pl.program_id(0) == 0)
+    def _():
+        flow_ref[...] = end_ref[...]
+        ga_ref[...] = jnp.zeros_like(ga_ref)
+
+    for group in range(0, channels, width):
+        pieces = [slice(at, at + LANES) for at in range(group, group + width, LANES)]
+        rates = [rate_ref[:, lanes] for lanes in pieces]
+        count = len(pieces)
+
+        def block(index, carried, last):
+            flows, sums, current = list(carried[:count]), list(carried[count:2*count]), list(carried[2*count:])
+            base = rows - UNROLL - index * UNROLL
+            steps = [tile(step_ref, base, lanes) for lanes in pieces]
+            pushes = [tile(push_ref, base, lanes) for lanes in pieces]
+            grads = [tile(grad_ref, base, lanes) for lanes in pieces]
+            alongs = [None] * count
+            slopes = [None] * count
+            for place in reversed(range(UNROLL)):
+                t = base + place
+                b_now = b_ref[t]
+                c_now = c_ref[t]
+                gb = gc = None
+                for k, lanes in enumerate(pieces):
+                    if last and place == 0:
+                        prior = first_ref[0, :, lanes].astype(jnp.float32)
+                    else:
+                        prior = kept_ref[t - 1, :, lanes].astype(jnp.float32)
+                    step = row(steps[k], place)
+                    grad = row(grads[k], place)
+                    decay = jnp.exp2(step * rates[k])
+                    adjoint = c_now * grad + flows[k]
+                    flows[k] = decay * adjoint
+                    decay_grad = flows[k] * prior
+                    alongs[k] = put_row(alongs[k], place, jnp.sum(adjoint * b_now, axis=0, keepdims=True))
+                    slopes[k] = put_row(slopes[k], place, jnp.sum(decay_grad * rates[k], axis=0, keepdims=True))
+                    sums[k] = sums[k] + decay_grad * step
+                    part_b = adjoint * row(pushes[k], place)
+                    part_c = current[k] * grad
+                    gb = part_b if gb is None else gb + part_b
+                    gc = part_c if gc is None else gc + part_c
+                    current[k] = prior
+                if group == 0:
+                    gb_ref[t] = gb
+                    gc_ref[t] = gc
+                else:
+                    gb_ref[t] += gb
+                    gc_ref[t] += gc
+            where = pl.ds(pl.multiple_of(base, UNROLL), UNROLL)
+            for k, lanes in enumerate(pieces):
+                along_ref[where, lanes] = alongs[k]
+                slope_ref[where, lanes] = slopes[k]
+            return tuple(flows + sums + current)
+
+        carried = (tuple(flow_ref[:, lanes] for lanes in pieces) + tuple(ga_ref[:, lanes] for lanes in pieces)
+                   + tuple(kept_ref[rows - 1, :, lanes].astype(jnp.float32) for lanes in pieces))
+        steps = rows // UNROLL
+        carried = lax.fori_loop(0, steps - 1, functools.partial(block, last=False), carried)
+        carried = block(steps - 1, carried, True)
+        for k, lanes in enumerate(pieces):
+            flow_ref[:, lanes] = carried[k]
+            ga_ref[:, lanes] = carried[count + k]
+
+def over_time(rows, width):
+    return pl.BlockSpec((rows, width), lambda i: (i, 0))
+
+PARAMS = pltpu.CompilerParams(vmem_limit_bytes=48 * 1024 * 1024, dimension_semantics=("arbitrary",))
+
+def pick(channels):
+    return 512 if channels % 512 == 0 else 128
+
+def scan_end(step, push, b_wide, rates, rows=64):
+    tokens, channels = step.shape
+    return pl.pallas_call(
+        functools.partial(end_kernel, pick(channels)),
+        grid=(tokens // rows,),
+        in_specs=[pl.BlockSpec((rows, channels), lambda i: (i, 0))] * 2
+        + [pl.BlockSpec((rows, NS, LANES), lambda i: (i, 0, 0)), pl.BlockSpec((NS, channels), lambda i: (0, 0))],
+        out_specs=pl.BlockSpec((NS, channels), lambda i: (0, 0)),
+        out_shape=jax.ShapeDtypeStruct((NS, channels), jnp.float32),
+        compiler_params=PARAMS,
+    )(step, push, b_wide, rates)
+
+def scan_out(step, push, b_wide, c_wide, rates, start, rows=64):
+    tokens, channels = step.shape
+    wide = pl.BlockSpec((rows, channels), lambda i: (i, 0))
+    cast = pl.BlockSpec((rows, NS, LANES), lambda i: (i, 0, 0))
+    fixed = pl.BlockSpec((NS, channels), lambda i: (0, 0))
+    return pl.pallas_call(
+        functools.partial(out_kernel, pick(channels)),
+        grid=(tokens // rows,),
+        in_specs=[wide, wide, cast, cast, fixed, fixed],
+        out_specs=[wide, pl.BlockSpec((rows, NS, channels), lambda i: (i, 0, 0)), pl.BlockSpec((1, NS, channels), lambda i: (i, 0, 0))],
+        out_shape=[jax.ShapeDtypeStruct((tokens, channels), jnp.float32),
+                   jax.ShapeDtypeStruct((tokens, NS, channels), jnp.bfloat16),
+                   jax.ShapeDtypeStruct((tokens // rows, NS, channels), jnp.bfloat16)],
+        scratch_shapes=[pltpu.VMEM((NS, channels), jnp.float32)],
+        compiler_params=PARAMS,
+    )(step, push, b_wide, c_wide, rates, start)
+
+def scan_inflow(step, grad, c_wide, rates, rows=64):
+    tokens, channels = step.shape
+    last = tokens // rows - 1
+    return pl.pallas_call(
+        functools.partial(inflow_kernel, pick(channels)),
+        grid=(tokens // rows,),
+        in_specs=[pl.BlockSpec((rows, channels), lambda i: (last - i, 0))] * 2
+        + [pl.BlockSpec((rows, NS, LANES), lambda i: (last - i, 0, 0)), pl.BlockSpec((NS, channels), lambda i: (0, 0))],
+        out_specs=pl.BlockSpec((NS, channels), lambda i: (0, 0)),
+        out_shape=jax.ShapeDtypeStruct((NS, channels), jnp.float32),
+        compiler_params=PARAMS,
+    )(step, grad, c_wide, rates)
+
+def scan_adjoint(step, push, grad, b_wide, c_wide, kept, firsts, rates, end, rows=64):
+    tokens, channels = step.shape
+    last = tokens // rows - 1
+    wide = pl.BlockSpec((rows, channels), lambda i: (last - i, 0))
+    cast = pl.BlockSpec((rows, NS, LANES), lambda i: (last - i, 0, 0))
+    fixed = pl.BlockSpec((NS, channels), lambda i: (0, 0))
+    return pl.pallas_call(
+        functools.partial(adjoint_kernel, pick(channels)),
+        grid=(tokens // rows,),
+        in_specs=[wide, wide, wide, cast, cast, pl.BlockSpec((rows, NS, channels), lambda i: (last - i, 0, 0)),
+                  pl.BlockSpec((1, NS, channels), lambda i: (last - i, 0, 0)), fixed, fixed],
+        out_specs=[wide, wide, cast, cast, fixed],
+        out_shape=[jax.ShapeDtypeStruct((tokens, channels), jnp.float32)] * 2
+        + [jax.ShapeDtypeStruct((tokens, NS, LANES), jnp.float32)] * 2
+        + [jax.ShapeDtypeStruct((NS, channels), jnp.float32)],
+        scratch_shapes=[pltpu.VMEM((NS, channels), jnp.float32)],
+        compiler_params=PARAMS,
+    )(step, push, grad, b_wide, c_wide, kept, firsts, rates, end)
 
 
 def shifted(value, axis, steps):
@@ -35,18 +276,6 @@
             + taps[:, offset][None, :] * ext_rows[offset : offset + length] * same_doc[:, None]
         )
     return result
-
-
-def forward_block(state_in, block_in, a_swap):
-    step_rows, b_rows, c_rows, xs_rows, keep_rows = block_in
-    decays = jnp.exp(step_rows[:, None, :] * a_swap[None]) * keep_rows[:, None, None]
-    pushes = b_rows[:, :, None] * (step_rows * xs_rows)[:, None, :]
-    states = []
-    state_now = state_in
-    for position in range(step_rows.shape[0]):
-        state_now = decays[position] * state_now + pushes[position]
-        states.append(state_now)
-    return (state_now, jnp.stack(states), decays)
 
 
 def body(
@@ -69,35 +298,34 @@
     expert_in,
     expert_out,
 ):
-    (
-        full_norm,
-        full_in,
-        full_taps,
-        full_bias,
-        full_xproj,
-        full_dt,
-        full_dtbias,
-        full_decay,
-        full_skip,
-        full_out,
-        full_moe,
-        full_router,
-    ) = (
-        lax.all_gather(norm_gain, ("ctx", "exp"), axis=0, tiled=True),
-        lax.all_gather(in_proj, ("ctx", "exp"), axis=0, tiled=True),
-        lax.all_gather(conv_taps, ("ctx", "exp"), axis=0, tiled=True),
-        lax.all_gather(conv_bias, ("ctx", "exp"), axis=0, tiled=True),
-        lax.all_gather(x_proj, ("ctx", "exp"), axis=0, tiled=True),
-        lax.all_gather(dt_proj, ("ctx", "exp"), axis=1, tiled=True),
-        lax.all_gather(dt_bias, ("ctx", "exp"), axis=0, tiled=True),
-        lax.all_gather(log_decay, ("ctx", "exp"), axis=0, tiled=True),
-        lax.all_gather(skip_gain, ("ctx", "exp"), axis=0, tiled=True),
-        lax.all_gather(out_proj, ("ctx", "exp"), axis=0, tiled=True),
-        lax.all_gather(moe_gain, ("ctx", "exp"), axis=0, tiled=True),
-        lax.all_gather(router, ("ctx", "exp"), axis=0, tiled=True),
-    )
+    everyone = ("ctx", "exp")
+    experts = router.shape[1]
+    half_rows = norm_gain.shape[0]
+    columns = (
+        x_proj,
+        dt_proj.T,
+        conv_taps,
+        conv_bias[:, None],
+        dt_bias[:, None],
+        log_decay,
+        skip_gain[:, None],
+        jnp.concatenate([norm_gain, moe_gain])[:, None],
+        router.reshape(2 * half_rows, experts // 2),
+    )
+    widths = [part.shape[1] for part in columns]
+    ends = [sum(widths[: k + 1]) for k in range(len(widths))]
+    full_small = lax.all_gather(jnp.concatenate(columns, axis=1), everyone, axis=0, tiled=True)
+    full_in = lax.all_gather(in_proj, everyone, axis=0, tiled=True)
+    full_out = lax.all_gather(out_proj, everyone, axis=0, tiled=True)
+    full_xproj, full_dt, full_taps, full_bias, full_dtbias, full_decay, full_skip, gains, full_router = [
+        full_small[:, end - width : end] for end, width in zip(ends, widths)
+    ]
+    full_dt = full_dt.T
+    full_bias, full_dtbias, full_skip = full_bias[:, 0], full_dtbias[:, 0], full_skip[:, 0]
+    gains = gains.reshape(-1, 2, half_rows)
+    full_norm, full_moe = gains[:, 0].reshape(-1), gains[:, 1].reshape(-1)
+    full_router = full_router.reshape(-1, experts)
     tokens_here = inputs.shape[1]
-    experts = router.shape[1]
     capacity = 5 * tokens_here // (4 * experts)
     flat_in = inputs[0].astype(jnp.float32)
     seg_row = segments[0]
@@ -135,36 +363,18 @@
     a_swap = -jnp.exp(full_decay.astype(jnp.float32)).T
     earlier = jnp.concatenate([prior_ids[KC - 2 :], seg_row[:-1]])
     keep_mask = (earlier == seg_row).astype(jnp.float32)
-    block_count = tokens_here // STATE_BLOCK
-
-    def split_rows(values):
-        return values.reshape((block_count, STATE_BLOCK) + values.shape[1:])
-
-    forward_inputs = (
-        split_rows(step_size),
-        split_rows(b_rows),
-        split_rows(c_rows),
-        split_rows(xs_wide),
-        split_rows(keep_mask),
-    )
-
-    def summary_pass(carried, block_in):
-        state_end, stacked, decays = forward_block(carried[0], block_in, a_swap)
-        return ((state_end, carried[1] * jnp.prod(decays, axis=0)), None)
-
+    masked_step = jnp.where(keep_mask[:, None] > 0, step_size, 1e30)
+    push = step_size * xs_wide
+    b_wide = jnp.broadcast_to(b_rows[:, :, None], (tokens_here, NS, LANES))
+    c_wide = jnp.broadcast_to(c_rows[:, :, None], (tokens_here, NS, LANES))
+    rates = a_swap * LOG2E
+    block_end = scan_end(masked_step, push, b_wide, rates)
+    block_product = jnp.exp2(jnp.sum(masked_step, axis=0)[None, :] * rates)
+    gathered = lax.all_gather(
+        jnp.stack([block_product, block_end]).astype(jnp.bfloat16)[None], "ctx", axis=0, tiled=True
+    ).astype(jnp.float32)
+    all_products, all_ends = gathered[:, 0], gathered[:, 1]
     zeros_state = jnp.zeros((NS, DI), jnp.float32)
-    ones_state = jnp.ones((NS, DI), jnp.float32)
-    (block_end, block_product), unused = lax.scan(
-        summary_pass, (zeros_state, ones_state), forward_inputs
-    )
-    all_products, all_ends = (
-        lax.all_gather(block_product[None].astype(jnp.bfloat16), "ctx", axis=0, tiled=True).astype(
-            jnp.float32
-        ),
-        lax.all_gather(block_end[None].astype(jnp.bfloat16), "ctx", axis=0, tiled=True).astype(
-            jnp.float32
-        ),
-    )
 
     def fold_start(index_now, start_now):
         return jnp.where(
@@ -173,15 +383,12 @@
             start_now,
         )
 
-    start_state = lax.fori_loop(0, all_products.shape[0], fold_start, zeros_state)
-
-    def output_pass(state_now, block_in):
-        state_end, stacked, decays = forward_block(state_now, block_in, a_swap)
-        return (state_end, (jnp.sum(stacked * block_in[2][:, :, None], axis=1), state_now))
-
-    unused_end, (scan_rows, block_starts) = lax.scan(output_pass, start_state, forward_inputs)
+    start_state = zeros_state
+    for index_now in range(all_products.shape[0]):
+        start_state = fold_start(index_now, start_state)
+    scan_rows, kept, firsts = scan_out(masked_step, push, b_wide, c_wide, rates, start_state)
     skip_wide = full_skip.astype(jnp.float32)
-    scanned_y = scan_rows.reshape(tokens_here, DI) + skip_wide * xs_wide
+    scanned_y = scan_rows + skip_wide * xs_wide
     gated_wide, gated_pull = jax.vjp(
         lambda scan_in, gate_in: scan_in * jax.nn.silu(gate_in), scanned_y, gate_z
     )
@@ -273,19 +480,7 @@
     grad_out_proj = jnp.dot(gated.T, grad_mixed, preferred_element_type=jnp.float32)
     grad_y, grad_z = gated_pull(grad_gated)
     grad_skip = jnp.sum(grad_y * xs_wide, axis=0)
-    grad_y_rows = split_rows(grad_y)
-
-    def zero_adjoint(inflow, block_in):
-        step_rows, b_part, c_part, xs_rows, keep_rows, grad_part = block_in
-        decays = jnp.exp(step_rows[:, None, :] * a_swap[None]) * keep_rows[:, None, None]
-        for place in reversed(range(step_rows.shape[0])):
-            adjoint = c_part[place][:, None] * grad_part[place][None, :] + inflow
-            inflow = decays[place] * adjoint
-        return (inflow, None)
-
-    local_inflow, unused_zero = lax.scan(
-        zero_adjoint, zeros_state, forward_inputs + (grad_y_rows,), reverse=True
-    )
+    local_inflow = scan_inflow(masked_step, grad_y, c_wide, rates)
     all_inflows = lax.all_gather(
         local_inflow[None].astype(jnp.bfloat16), "ctx", axis=0, tiled=True
     ).astype(jnp.float32)
@@ -297,34 +492,17 @@
             source > position, all_inflows[source] + all_products[source] * end_now, end_now
         )
 
-    end_inflow = lax.fori_loop(0, total_ctx, fold_end, zeros_state)
-
-    def full_adjoint(inflow, block_in):
-        step_rows, b_part, c_part, xs_rows, keep_rows, grad_part, start_in = block_in
-        state_end, stacked, decays = forward_block(
-            start_in, (step_rows, b_part, c_part, xs_rows, keep_rows), a_swap
-        )
-        previous = jnp.concatenate([start_in[None], stacked[:-1]], axis=0)
-        adjoints = []
-        for place in reversed(range(step_rows.shape[0])):
-            adjoint = c_part[place][:, None] * grad_part[place][None, :] + inflow
-            inflow = decays[place] * adjoint
-            adjoints.append(adjoint)
-        adjoint_stack = jnp.stack(adjoints[::-1])
-        decay_grad = adjoint_stack * previous * decays
-        along_b = jnp.sum(adjoint_stack * b_part[:, :, None], axis=1)
-        grad_step = along_b * xs_rows + jnp.sum(decay_grad * a_swap[None], axis=1)
-        grad_b = jnp.sum(adjoint_stack * (step_rows * xs_rows)[:, None, :], axis=2)
-        grad_xs = along_b * step_rows
-        grad_c = jnp.sum(stacked * grad_part[:, None, :], axis=2)
-        grad_a = jnp.sum(decay_grad * step_rows[:, None, :], axis=0)
-        return (inflow, (grad_step, grad_b, grad_xs, grad_c, grad_a))
-
-    unused_in, (grad_steps, grad_bs, grad_xss, grad_cs, grad_as) = lax.scan(
-        full_adjoint, end_inflow, forward_inputs + (grad_y_rows, block_starts), reverse=True
-    )
-    grad_step_all = grad_steps.reshape(tokens_here, DI)
-    grad_log_decay = (jnp.sum(grad_as, axis=0) * a_swap).T
+    end_inflow = zeros_state
+    for step_index in range(total_ctx):
+        end_inflow = fold_end(step_index, end_inflow)
+    along_b, slope, wide_b, wide_c, grad_a = scan_adjoint(
+        masked_step, push, grad_y, b_wide, c_wide, kept, firsts, rates, end_inflow
+    )
+    grad_step_all = along_b * xs_wide + slope * (1.0 / LOG2E)
+    grad_xss = along_b * step_size
+    grad_bs = jnp.sum(wide_b, axis=2)
+    grad_cs = jnp.sum(wide_c, axis=2)
+    grad_log_decay = (grad_a * a_swap).T
     soft_slope = jax.nn.sigmoid(dt_pre)
     grad_pre_wide = grad_step_all * soft_slope
     grad_dt_bias = jnp.sum(grad_pre_wide, axis=0)
@@ -332,12 +510,12 @@
     grad_dt_proj = jnp.dot(delta_low.T, grad_dt_pre, preferred_element_type=jnp.float32)
     grad_delta = jnp.dot(grad_dt_pre, full_dt.T, preferred_element_type=jnp.float32)
     grad_projected = jnp.concatenate(
-        [grad_delta, grad_bs.reshape(tokens_here, NS), grad_cs.reshape(tokens_here, NS)], axis=1
+        [grad_delta, grad_bs, grad_cs], axis=1
     ).astype(jnp.bfloat16)
     grad_x_proj = jnp.dot(xs_val.T, grad_projected, preferred_element_type=jnp.float32)
     grad_xs_total = (
         skip_wide * grad_y
-        + grad_xss.reshape(tokens_here, DI)
+        + grad_xss
         + jnp.dot(grad_projected, full_xproj.T, preferred_element_type=jnp.float32)
     )
     grad_conv = silu_pull(grad_xs_total)[0]
@@ -351,35 +529,44 @@
     grad_normed_one = jnp.dot(grad_mixed_in, full_in.T, preferred_element_type=jnp.float32)
     grad_inputs_norm, grad_norm_gain = norm_one_pull(grad_normed_one)
     grad_inputs = grad_resid + grad_inputs_norm
-    shares = (
-        lax.psum_scatter(grad_norm_gain, ("ctx", "exp"), scatter_dimension=0, tiled=True),
-        lax.psum_scatter(grad_in_proj, ("ctx", "exp"), scatter_dimension=0, tiled=True),
-        lax.psum_scatter(grad_taps, ("ctx", "exp"), scatter_dimension=0, tiled=True),
-        lax.psum_scatter(grad_cbias, ("ctx", "exp"), scatter_dimension=0, tiled=True),
-        lax.psum_scatter(grad_x_proj, ("ctx", "exp"), scatter_dimension=0, tiled=True),
-        lax.psum_scatter(grad_dt_proj, ("ctx", "exp"), scatter_dimension=1, tiled=True),
-        lax.psum_scatter(grad_dt_bias, ("ctx", "exp"), scatter_dimension=0, tiled=True),
-        lax.psum_scatter(grad_log_decay, ("ctx", "exp"), scatter_dimension=0, tiled=True),
-        lax.psum_scatter(grad_skip, ("ctx", "exp"), scatter_dimension=0, tiled=True),
-        lax.psum_scatter(grad_out_proj, ("ctx", "exp"), scatter_dimension=0, tiled=True),
-        lax.psum_scatter(grad_moe_gain, ("ctx", "exp"), scatter_dimension=0, tiled=True),
-        lax.psum_scatter(grad_router, ("ctx", "exp"), scatter_dimension=0, tiled=True),
-    )
+    sums = (
+        grad_x_proj,
+        grad_dt_proj.T,
+        grad_taps,
+        grad_cbias[:, None],
+        grad_dt_bias[:, None],
+        grad_log_decay,
+        grad_skip[:, None],
+        jnp.stack(
+            [grad_norm_gain.reshape(-1, half_rows), grad_moe_gain.reshape(-1, half_rows)], axis=1
+        ).reshape(-1, 1),
+        grad_router.reshape(-1, experts // 2),
+    )
+
+    def scatter(values):
+        return lax.psum_scatter(values, everyone, scatter_dimension=0, tiled=True)
+
+    own_in = scatter(grad_in_proj.astype(jnp.bfloat16)).astype(jnp.float32)
+    own_out = scatter(grad_out_proj.astype(jnp.bfloat16)).astype(jnp.float32)
+    own_small = scatter(jnp.concatenate(sums, axis=1))
+    own_x, own_dt, own_taps, own_bias, own_dtbias, own_decay, own_skip, own_gains, own_router = [
+        own_small[:, end - width : end] for end, width in zip(ends, widths)
+    ]
     return (
         out_block,
         grad_inputs[None],
-        shares[0],
-        shares[1],
-        shares[2],
-        shares[3],
-        shares[4],
-        shares[5],
-        shares[6],
-        shares[7],
-        shares[8],
-        shares[9],
-        shares[10],
-        shares[11],
+        own_gains[:half_rows, 0],
+        own_in,
+        own_taps,
+        own_bias[:, 0],
+        own_x,
+        own_dt.T,
+        own_dtbias[:, 0],
+        own_decay,
+        own_skip[:, 0],
+        own_out,
+        own_gains[half_rows:, 0],
+        own_router.reshape(half_rows, experts),
         grad_w_in,
         grad_w_out,
     )

time: 3100 us -> 855 us (0.28); the launches traced: 3060 us -> 846 us
  other arithmetic: 1380 us -> 56.6 us
  blocking collectives: 464 us -> 117 us
  local copies, waits for them, and re-layouts: 392 us -> 51.7 us
  waiting for transfers between devices: 693 us -> 425 us
  Pallas kernels: 0 us -> 70.6 us
    while x744 -> x0, other arithmetic: 1010 us -> none
    all_gather x7 -> x2, blocking collectives: 355 us -> 87 us  [the longest x1 75.5 us: body(): lax.all_gather(jnp.concatenate(columns, axis=1), everyone, axis=0, tiled=...]
    mul x180 -> x0, local copies, waits for them, and re-layouts: 189 us -> none  [the longest x24 38.8 us: zero_adjoint(): adjoint = c_part[place][:, None] * grad_part[place][None, :] + inflow]
    reduce_scatter x3 -> x2, waiting for transfers between devices: 352 us -> 203 us  [scatter(): return lax.psum_scatter(values, everyone, scatter_dimension=0, tiled=True)]
    unnamed x15 -> x10, waiting for transfers between devices: 204 us -> 70.3 us
    slice x49 -> x10, local copies, waits for them, and re-layouts: 107 us -> 7.08 us  [the longest x5 4.77 us: body(): own_small[:, end - width:end]]
    mul x133 -> x1, other arithmetic: 95.1 us -> 0.01 us  [body(): block_product = jnp.exp2(jnp.sum(masked_step, axis=0)[None, :] * rates)]
    reduce_sum x37 -> x2, other arithmetic: 93.6 us -> 5.73 us  [the longest x1 2.94 us: body(): grad_cs = jnp.sum(wide_c, axis=2)]
  transfers between devices with their start and end apart: 18 -> 15, of which waited for: 11 -> 10; matrix products, arithmetic and copies ran while one was open for 22% -> 13% of each run, Pallas kernels for 0% -> 3%
where the time goes in v1:
time: 855 us; the launch traced here: 846 us
  waiting for transfers between devices  425 us (50%)
  blocking collectives  117 us (14%)
  matrix products  91.9 us (11%)
  Pallas kernels  70.6 us (8%)
  other arithmetic  56.6 us (7%)
  local copies, waits for them, and re-layouts  51.7 us (6%)
  starting transfers between devices  17.8 us (2%)
  between operations  16 us (2%)
    reduce_scatter x2, waiting for transfers between devices, scatter(): return lax.psum_scatter(values, everyone, scatter_dimension=0, tiled=True)  203 us
    all_gather x1, blocking collectives, body(): lax.all_gather(jnp.concatenate(columns, axis=1), everyone, axis=0, tiled=...  75.5 us
    unnamed x10, waiting for transfers between devices  70.3 us
    reduce_scatter x1, waiting for transfers between devices, body(): lax.psum_scatter(grad_expert_out[None].astype(jnp.bfloat16), 'ctx', scatt...  47.8 us
    reduce_scatter x1, waiting for transfers between devices, body(): lax.psum_scatter(grad_expert_in[None].astype(jnp.bfloat16), 'ctx', scatte...  47.7 us
    pallas_call x1, Pallas kernels, scan_adjoint(): pl.pallas_call(functools.partial(adjoint_kernel, pick(channels)), grid=(t...  34.7 us
    all_to_all x1, blocking collectives, body(): lax.all_to_all(grad_buffer, 'exp', split_axis=0, concat_axis=0, tiled=True)  23.9 us
    unnamed x237, local copies, waits for them, and re-layouts  23.2 us
  transfers between devices with their start and end apart: 15, of which 10 were waited for; matrix products, arithmetic and copies ran while one was open for 13% of the time, Pallas kernels for 3%

profile of v1, /device:TPU:0, one launch (start us, length us, event | category | flops | bytes accessed | tf_op | source)
XLA Modules:
  0.0 846.0 jit_solution(18266145772063181265)
XLA Ops:
  13.8 75.5 %all_gather.21 = bf16[1536,156]{1,0:T(8,128)(2,1)S(1)} all-gather(bf16[48,156]{1,0:T(8,128)(2,1)S(1)} %concatenate.46), channel_id=1, replica_groups=mesh['ctx'=4,'exp'=8] {'ctx','exp'}, dimensions={0}, use_global_device_ids=true | all-gather | bytes 494208 | tf_op jit(solution)/shard_map/all_gather | solution.py:317
  96.9 6.5 fusion.126
  106.1 3.2 multiply_convert_fusion.2
  112.5 4.7 fusion.120
  117.2 2.6 broadcast_in_dim.59.b_ref
  119.8 8.5 %shard_map.297 = f32[16,1536]{1,0:T(8,128)S(1)} custom-call(f32[384,1536]{1,0:T(8,128)S(1)} %get-tuple-element.125.step_ref, f32[384,1536]{1,0:T(8,128)S(1)} %get-tuple-element.133.push_ref, f32[384,16,128]{2,1,0:T(8,128)} %broadcast_in_dim.59.b_ref, f32[16,1536]{1,0:T(8,128)S(1)} %get-tuple-element.148.rate_ref), custom_call_target="tpu_custom_call" | custom-call | tf_op jit(solution)/shard_map/pallas_call | solution.py:198
  128.3 11.4 %all_gather.23 = bf16[4,2,16,1536]{3,2,1,0:T(8,128)(2,1)S(1)} all-gather(bf16[1,2,16,1536]{3,2,1,0:T(8,128)(2,1)S(1)} %pad_maximum_fusion.3), channel_id=1, replica_groups=mesh['ctx'=4,'exp'=8] {'ctx'}, dimensions={0}, use_global_device_ids=true | all-gather | bytes 491520 | tf_op jit(solution)/shard_map/all_gather | solution.py:373
  142.0 18.3 %shard_map.298 = (f32[384,1536]{1,0:T(8,128)S(1)}, bf16[384,16,1536]{2,1,0:T(8,128)(2,1)}, bf16[6,16,1536]{2,1,0:T(8,128)(2,1)S(1)}) custom-call(f32[384,1536]{1,0:T(8,128)S(1)} %get-tuple-element.125.step_ref, f32[384,1536]{1,0:T(8,128)} %copy-done.1, f32[384,16,128]{2,1,0:T(8,128)} %broadcast_in_dim.59.b_ref, f32[384,16,128]{2,1,0:T(8,128)} %broadcast_in_dim.60.c_ref, ...), custom_call_target="tpu_custom_call" | custom-call | tf_op jit(solution)/shard_map/pallas_call | solution.py:213
  163.7 4.2 multiply_reduce_fusion.6
  167.9 3.2 scatter_custom_fusion
  172.1 3.5 all-to-all-start
  175.7 2.9 all-gather.10.cloned.1.call-done
  178.5 18.0 %all-to-all-done = bf16[8,60,768]{2,1,0:T(8,128)(2,1)S(1)} async-done(((bf16[8,60,768]{2,1,0:T(8,128)(2,1)}), bf16[8,60,768]{2,1,0:T(8,128)(2,1)S(1)}, u32[]{:S(2)}, u32[]{:S(2)}) %all-to-all-start) | async-done | bytes 737312 | tf_op jit(solution)/shard_map/all_to_all | solution.py:421
  196.5 6.1 fusion.30
  202.7 2.7 copy-done.14
  205.3 15.1 %multiply_convert_fusion = (bf16[8,60,3072]{2,1,0:T(8,128)(2,1)}, f32[8,60,3072]{2,1,0:T(8,128)}) fusion(f32[8,60,3072]{2,1,0:T(8,128)S(1)} %get-tuple-element.158, u8[60,3072]{1,0:T(8,128)(4,1)S(1)} %get-tuple-element.97, u8[60,3072]{1,0:T(8,128)(4,1)S(1)} %get-tuple-element.96), kind=kLoop, calls=%fused_computation.15 | loop fusion | flops 103219200 | bytes 15114240 | tf_op jit(solution)/shard_map/convert_element_type | solution.py:423
  220.4 6.8 fusion.37
  227.2 4.4 all-to-all-start.1
  234.6 17.2 %all-to-all-done.1 = bf16[8,60,768]{2,1,0:T(8,128)(2,1)} async-done(((bf16[8,60,768]{2,1,0:T(8,128)(2,1)}), bf16[8,60,768]{2,1,0:T(8,128)(2,1)}, u32[]{:S(2)}, u32[]{:S(2)}) %all-to-all-start.1) | async-done | bytes 737312 | tf_op jit(solution)/shard_map/all_to_all | solution.py:428
  253.1 2.6 gather_fusion
  258.4 3.7 scatter_custom_fusion.1
  263.3 23.9 %all_to_all.20 = bf16[8,60,768]{2,1,0:T(8,128)(2,1)S(1)} all-to-all(bf16[8,60,768]{2,1,0:T(8,128)(2,1)S(1)} %reshape.310), channel_id=1, replica_groups=mesh['ctx'=4,'exp'=8] {'exp'}, dimensions={0} | all-to-all | bytes 1474560 | tf_op jit(solution)/shard_map/all_to_all | solution.py:441
  287.2 8.6 %add_convert_fusion = bf16[8,60,3072]{2,1,0:T(8,128)(2,1)S(1)} fusion(f32[8,60,3072]{2,1,0:T(8,128)} %get-tuple-element.123, f32[8,60,3072]{2,1,0:T(8,128)} %copy-done.14, bf16[8,60,768]{2,1,0:T(8,128)(2,1)S(1)} %all_to_all.20, bf16[1,3072,768]{2,1,0:T(8,128)(2,1)} %all-gather.12.cloned.1.call-done), kind=kOutput, calls=%fused_computation.14 | convolution fusion | flops 2285568000 | bytes 20201472 | tf_op jit(solution)/shard_map/srd,fd->srf/dot_general | solution.py:442
  297.5 3.6 fusion.34
  301.1 4.2 all-to-all-start.3
  308.6 16.1 %all-to-all-done.3 = bf16[8,60,768]{2,1,0:T(8,128)(2,1)} async-done(((bf16[8,60,768]{2,1,0:T(8,128)(2,1)}), bf16[8,60,768]{2,1,0:T(8,128)(2,1)}, u32[]{:S(2)}, u32[]{:S(2)}) %all-to-all-start.3) | async-done | bytes 737312 | tf_op jit(solution)/shard_map/all_to_all | solution.py:458
  326.0 2.8 gather_fusion.1
  328.9 2.8 multiply_reduce_fusion.4
  334.0 5.4 fusion.26
  339.4 9.1 %shard_map.299 = f32[16,1536]{1,0:T(8,128)S(1)} custom-call(f32[384,1536]{1,0:T(8,128)S(1)} %get-tuple-element.125.step_ref, f32[384,1536]{1,0:T(8,128)S(1)} %get-tuple-element.119.grad_ref, f32[384,16,128]{2,1,0:T(8,128)} %broadcast_in_dim.60.c_ref, f32[16,1536]{1,0:T(8,128)S(1)} %get-tuple-element.148.rate_ref), custom_call_target="tpu_custom_call" | custom-call | tf_op jit(solution)/shard_map/pallas_call | solution.py:228
  348.5 5.8 all-gather
  354.4 34.7 %shard_map.300 = (f32[384,1536]{1,0:T(8,128)S(1)}, f32[384,1536]{1,0:T(8,128)S(1)}, f32[384,16,128]{2,1,0:T(8,128)}, f32[384,16,128]{2,1,0:T(8,128)}, f32[16,1536]{1,0:T(8,128)S(1)}) custom-call(f32[384,1536]{1,0:T(8,128)} %copy-done, f32[384,1536]{1,0:T(8,128)} %copy-done.1, f32[384,1536]{1,0:T(8,128)} %copy-done.2, ...), custom_call_target="tpu_custom_call" | custom-call | tf_op jit(solution)/shard_map/pallas_call | solution.py:244
  392.6 2.8 reduce_sum.198
  395.4 2.9 reduce_sum.202
  398.6 2.4 fusion.90
  401.1 8.6 %multiply_reduce_fusion.3 = (f32[1536]{0:T(1024)S(1)}, f32[1536]{0:T(1024)S(1)}, f32[1536]{0:T(1024)S(1)}, f32[1536]{0:T(1024)S(1)}, f32[1536]{0:T(1024)S(1)}, /...) fusion(f32[387,1536]{1,0:T(8,128)} %copy-done.7, ...), kind=kOutput, calls=%fused_computation.69 | convolution fusion | flops 115192320 | bytes 28844032 | tf_op jit(solution)/shard_map/dot_general | solution.py:519
  414.5 5.9 fusion.41
  422.8 4.1 convolution_convert_fusion.1
  428.2 5.7 convolution_convert_fusion
  435.1 6.8 fusion.15
  443.0 6.2 fusion.14
  451.8 68.2 %reduce-scatter.16.cloned.1.call-done = f32[48,156]{1,0:T(8,128)} async-done(((f32[1536,156]{1,0:T(8,128)}), f32[48,156]{1,0:T(8,128)}) %reduce-scatter.16.cloned.1.call-update) | async-done | bytes 29968
  531.2 92.5 %reduce-scatter.10.cloned.1.call-done = bf16[48,768]{1,0:T(8,128)(2,1)} async-done(((bf16[1536,768]{1,0:T(8,128)(2,1)}), bf16[48,768]{1,0:T(8,128)(2,1)}) %reduce-scatter.10.cloned.1.call-update) | async-done | bytes 73744 | tf_op jit(solution)/shard_map/reduce_scatter | solution.py:547
  625.3 110.8 %reduce-scatter.8.cloned.1.call-done = bf16[24,3072]{1,0:T(8,128)(2,1)} async-done(((bf16[768,3072]{1,0:T(8,128)(2,1)}), bf16[24,3072]{1,0:T(8,128)(2,1)}) %reduce-scatter.8.cloned.1.call-update) | async-done | bytes 147472 | tf_op jit(solution)/shard_map/reduce_scatter | solution.py:547
  737.8 47.8 %reduce-scatter.14.cloned.1.call-done = bf16[1,768,768]{2,1,0:T(8,128)(2,1)} async-done(((bf16[1,3072,768]{2,1,0:T(8,128)(2,1)}), bf16[1,768,768]{2,1,0:T(8,128)(2,1)}) %reduce-scatter.14.cloned.1.call-update) | async-done | bytes 1179664 | tf_op jit(solution)/shard_map/reduce_scatter | solution.py:464
  785.6 2.8 convert_element_type.256
  788.4 47.7 %reduce-scatter.12.cloned.1.call-done = bf16[1,768,768]{2,1,0:T(8,128)(2,1)} async-done(((bf16[1,768,3072]{2,1,0:T(8,128)(2,1)}), bf16[1,768,768]{2,1,0:T(8,128)(2,1)}) %reduce-scatter.12.cloned.1.call-update) | async-done | bytes 1179664 | tf_op jit(solution)/shard_map/reduce_scatter | solution.py:461
  836.2 2.8 convert_element_type.253
  (367 shorter events, 73.9 us)
Async XLA Ops:
  7.3 89.7 %all-gather.6.cloned.1.call-start = ((), (), s32[]{:S(2)}) async-start(), calls=%async_computation.9 | async-start | bytes 4866048 | tf_op jit(solution)/shard_map/all_gather | solution.py:318
  8.0 155.7 %all-gather.8.cloned.1.call-start = ((), (), s32[]{:S(2)}) async-start(), calls=%async_computation.10 | async-start | bytes 2433024 | tf_op jit(solution)/shard_map/all_gather | solution.py:319
  8.8 169.8 %all-gather.10.cloned.1.call-start = ((), (), s32[]{:S(2)}) async-start(), calls=%async_computation.11 | async-start | bytes 5898240 | tf_op jit(solution)/shard_map/all_gather | solution.py:416
  9.5 210.9 %all-gather.12.cloned.1.call-start = ((), (), s32[]{:S(2)}) async-start(), calls=%async_computation.12 | async-start | bytes 5898240 | tf_op jit(solution)/shard_map/all_gather | solution.py:417
  10.3 86.0 %collective-permute-start = (bf16[3]{0:T(256)(128)(2,1)S(1)}, bf16[3]{0:T(256)(128)(2,1)S(1)}, u32[]{:S(2)}, u32[]{:S(2)}) collective-permute-start(bf16[3]{0:T(256)(128)(2,1)S(1)} %fusion.106), channel_id=1, source_target_pairs={{0,8},{8,16},{16,24},{1,9},{9,17},{17,25},{2,10},{10,18},{18,26},{... | collective-permute-start | bytes 26 | tf_op jit(solution)/shard_map/ppermute | solution.py:261
  89.4 23.1 %copy-start.11 = (bf16[1536,156]{1,0:T(8,128)(2,1)}, bf16[1536,156]{1,0:T(8,128)(2,1)S(1)}, u32[]{:S(2)}) copy-start(bf16[1536,156]{1,0:T(8,128)(2,1)S(1)} %all_gather.21) | copy-start | bytes 1437700
  90.9 69.4 %copy-start.59 = (f32[1536]{0:T(1024)}, f32[1536]{0:T(1024)S(1)}, u32[]{:S(2)}) copy-start(f32[1536]{0:T(1024)S(1)} %get-tuple-element.107) | copy-start | bytes 18436
  92.3 11.2 %copy-start.71 = (f32[384]{0:T(512)}, f32[384]{0:T(512)S(1)}, u32[]{:S(2)}) copy-start(f32[384]{0:T(512)S(1)} %fusion.48) | copy-start | bytes 4612
  92.3 11.2 %copy-start.88 = (f32[384]{0:T(512)}, f32[384]{0:T(512)S(1)}, u32[]{:S(2)}) copy-start(f32[384]{0:T(512)S(1)} %fusion.103) | copy-start | bytes 4612
  94.5 8.9 %copy-start.77 = (f32[768]{0:T(1024)}, f32[768]{0:T(1024)S(1)}, u32[]{:S(2)}) copy-start(f32[768]{0:T(1024)S(1)} %reshape.317) | copy-start | bytes 9220
  94.7 22.4 %copy-start.41 = (bf16[1536,16]{0,1:T(8,128)(2,1)}, bf16[1536,16]{0,1:T(8,128)(2,1)S(1)}, u32[]{:S(2)}) copy-start(bf16[1536,16]{0,1:T(8,128)(2,1)S(1)} %copy.91) | copy-start | bytes 147460
  96.2 9.8 %copy-start.61 = (f32[1536]{0:T(1024)}, f32[1536]{0:T(1024)S(1)}, u32[]{:S(2)}) copy-start(f32[1536]{0:T(1024)S(1)} %get-tuple-element.110) | copy-start | bytes 18436
  96.2 9.8 %copy-start.63 = (f32[1536]{0:T(1024)}, f32[1536]{0:T(1024)S(1)}, u32[]{:S(2)}) copy-start(f32[1536]{0:T(1024)S(1)} %get-tuple-element.111) | copy-start | bytes 18436
  96.2 9.8 %copy-start.65 = (f32[1536]{0:T(1024)}, f32[1536]{0:T(1024)S(1)}, u32[]{:S(2)}) copy-start(f32[1536]{0:T(1024)S(1)} %get-tuple-element.112) | copy-start | bytes 18436
  96.3 9.8 %copy-start.67 = (f32[1536]{0:T(1024)}, f32[1536]{0:T(1024)S(1)}, u32[]{:S(2)}) copy-start(f32[1536]{0:T(1024)S(1)} %get-tuple-element.113) | copy-start | bytes 18436
  103.5 2.1 collective-permute-start.1
  117.1 11.1 %copy-start.1 = (f32[384,1536]{1,0:T(8,128)}, f32[384,1536]{1,0:T(8,128)S(1)}, u32[]{:S(2)}) copy-start(f32[384,1536]{1,0:T(8,128)S(1)} %get-tuple-element.133.push_ref) | copy-start | bytes 7077892
  117.1 222.2 %copy-start = (f32[384,1536]{1,0:T(8,128)}, f32[384,1536]{1,0:T(8,128)S(1)}, u32[]{:S(2)}) copy-start(f32[384,1536]{1,0:T(8,128)S(1)} %get-tuple-element.125.step_ref) | copy-start | bytes 7077892
  139.8 20.6 %copy-start.19 = (f32[4,2,16,1536]{3,2,1,0:T(8,128)}, f32[4,2,16,1536]{3,2,1,0:T(8,128)S(1)}, u32[]{:S(2)}) copy-start(f32[4,2,16,1536]{3,2,1,0:T(8,128)S(1)} %convert_element_type.223) | copy-start | bytes 2359300
  139.9 22.0 %slice-start = ((s8[4718592]{0:T(1024)(128)(4,1)}), s8[4194304]{0:T(1024)(128)(4,1)S(1)}, s32[]{:S(2)}) async-start(s8[4718592]{0:T(1024)(128)(4,1)} %bitcast.181), calls=%async_computation.18 | async-start | bytes 8388608
  142.0 19.8 %copy-start.9 = (bf16[384,1536]{1,0:T(8,128)(2,1)S(1)}, bf16[384,1536]{1,0:T(8,128)(2,1)}, u32[]{:S(2)}) copy-start(bf16[384,1536]{1,0:T(8,128)(2,1)} %copy-done.8) | copy-start | bytes 3538948
  142.0 19.8 %slice-start.1 = ((s8[4718592]{0:T(1024)(128)(4,1)}), s8[524288]{0:T(1024)(128)(4,1)S(1)}, s32[]{:S(2)}) async-start(s8[4718592]{0:T(1024)(128)(4,1)} %bitcast.181), calls=%async_computation.19 | async-start | bytes 1048576
  167.9 64.0 %copy-start.48 = (f32[384]{0:T(512)}, f32[384]{0:T(512)S(1)}, u32[]{:S(2)}) copy-start(f32[384]{0:T(512)S(1)} %fusion.104) | copy-start | bytes 4612
  172.1 24.4 %all-to-all-start = ((bf16[8,60,768]{2,1,0:T(8,128)(2,1)}), bf16[8,60,768]{2,1,0:T(8,128)(2,1)S(1)}, u32[]{:S(2)}, u32[]{:S(2)}) async-start(bf16[8,60,768]{2,1,0:T(8,128)(2,1)} %reshape.308), calls=%async_computation | async-start | bytes 1572864 | tf_op jit(solution)/shard_map/all_to_all | solution.py:421
  220.4 11.2 %copy-start.29 = (bf16[1536,4]{1,0:T(8,128)(2,1)S(1)}, bf16[1536,4]{1,0:T(8,128)(2,1)}, u32[]{:S(2)}) copy-start(bf16[1536,4]{1,0:T(8,128)(2,1)} %get-tuple-element.136) | copy-start | bytes 36868
  227.2 24.6 %all-to-all-start.1 = ((bf16[8,60,768]{2,1,0:T(8,128)(2,1)}), bf16[8,60,768]{2,1,0:T(8,128)(2,1)}, u32[]{:S(2)}, u32[]{:S(2)}) async-start(bf16[8,60,768]{2,1,0:T(8,128)(2,1)} %fusion.37), calls=%async_computation.1 | async-start | bytes 1572864 | tf_op jit(solution)/shard_map/all_to_all | solution.py:428
  231.9 21.2 %copy-start.75 = (s32[1024]{0:T(1024)}, s32[1024]{0:T(1024)S(1)}, u32[]{:S(2)}) copy-start(s32[1024]{0:T(1024)S(1)} %pad_clamp_fusion) | copy-start | bytes 12292
  234.5 22.7 %copy-start.50 = (f32[384]{0:T(512)}, f32[384]{0:T(512)S(1)}, u32[]{:S(2)}) copy-start(f32[384]{0:T(512)S(1)} %get-tuple-element.159) | copy-start | bytes 4612
  234.5 22.7 %copy-start.56 = (f32[384]{0:T(512)}, f32[384]{0:T(512)S(1)}, u32[]{:S(2)}) copy-start(f32[384]{0:T(512)S(1)} %fusion.99) | copy-start | bytes 4612
  263.3 34.2 %slice-start.2 = ((s8[4718592]{0:T(1024)(128)(4,1)}), s8[4194304]{0:T(1024)(128)(4,1)S(1)}, s32[]{:S(2)}) async-start(s8[4718592]{0:T(1024)(128)(4,1)} %bitcast.195), calls=%async_computation.20 | async-start | bytes 8388608
  287.2 8.6 %copy-start.37 = (bf16[8,60,768]{2,1,0:T(8,128)(2,1)}, bf16[8,60,768]{2,1,0:T(8,128)(2,1)S(1)}, u32[]{:S(2)}) copy-start(bf16[8,60,768]{2,1,0:T(8,128)(2,1)S(1)} %all_to_all.20) | copy-start | bytes 2211844
  287.2 10.3 %slice-start.3 = ((s8[4718592]{0:T(1024)(128)(4,1)}), s8[524288]{0:T(1024)(128)(4,1)S(1)}, s32[]{:S(2)}) async-start(s8[4718592]{0:T(1024)(128)(4,1)} %bitcast.195), calls=%async_computation.21 | async-start | bytes 1048576
  297.5 7.9 copy-start.18
  297.5 7.9 copy-start.46
  297.5 7.9 copy-start.51
  297.5 7.9 copy-start.54
  297.5 7.9 copy-start.57
  297.5 7.9 copy-start.73
  301.1 23.6 %all-to-all-start.3 = ((bf16[8,60,768]{2,1,0:T(8,128)(2,1)}), bf16[8,60,768]{2,1,0:T(8,128)(2,1)}, u32[]{:S(2)}, u32[]{:S(2)}) async-start(bf16[8,60,768]{2,1,0:T(8,128)(2,1)} %fusion.34), calls=%async_computation.3 | async-start | bytes 1572864 | tf_op jit(solution)/shard_map/all_to_all | solution.py:458
  305.3 214.7 %reduce-scatter.16.cloned.1.call-start = ((), (), s32[]{:S(2)}) async-start(), calls=%async_computation.17 | async-start | bytes 1622016
  339.4 9.1 %copy-start.2 = (f32[384,1536]{1,0:T(8,128)}, f32[384,1536]{1,0:T(8,128)S(1)}, u32[]{:S(2)}) copy-start(f32[384,1536]{1,0:T(8,128)S(1)} %get-tuple-element.119.grad_ref) | copy-start | bytes 7077892
  339.4 15.0 %copy-start.20 = (f32[4,2,16,1536]{3,2,1,0:T(8,128)S(1)}, f32[4,2,16,1536]{3,2,1,0:T(8,128)}, u32[]{:S(2)}) copy-start(f32[4,2,16,1536]{3,2,1,0:T(8,128)} %copy-done.19) | copy-start | bytes 2359300
  354.4 34.7 %copy-start.26 = (f32[384,1536]{1,0:T(8,128)S(1)}, f32[384,1536]{1,0:T(8,128)}, u32[]{:S(2)}) copy-start(f32[384,1536]{1,0:T(8,128)} %get-tuple-element.155) | copy-start | bytes 7077892
  410.9 3.2 collective-permute-start.2
  422.8 201.0 %reduce-scatter.10.cloned.1.call-start = ((), (), s32[]{:S(2)}) async-start(), calls=%async_computation.14 | async-start | bytes 2433024 | tf_op jit(solution)/shard_map/reduce_scatter | solution.py:547
  426.9 309.2 %reduce-scatter.8.cloned.1.call-start = ((), (), s32[]{:S(2)}) async-start(), calls=%async_computation.13 | async-start | bytes 4866048 | tf_op jit(solution)/shard_map/reduce_scatter | solution.py:547
  433.9 351.7 %reduce-scatter.14.cloned.1.call-start = ((), (), s32[]{:S(2)}) async-start(), calls=%async_computation.16 | async-start | bytes 5898240 | tf_op jit(solution)/shard_map/reduce_scatter | solution.py:464
  441.9 394.3 %reduce-scatter.12.cloned.1.call-start = ((), (), s32[]{:S(2)}) async-start(), calls=%async_computation.15 | async-start | bytes 5898240 | tf_op jit(solution)/shard_map/reduce_scatter | solution.py:461
  (78 other events, 271.5 us)
Sparse Core Ops, SparseCore 0:
  11.0 68.9 all-gather.5
  82.9 57.6 all-gather.7
  142.1 36.3 all-gather.9
  180.0 37.4 all-gather.11
  422.9 97.0 reduce-scatter.15
  525.7 97.9 reduce-scatter.9
  630.1 105.9 reduce-scatter.7
  738.6 46.9 reduce-scatter.13
  788.3 47.8 reduce-scatter.11

commit v2 on v1

--- a/solution.py
+++ b/solution.py
@@ -18,6 +18,7 @@
 
 
 EPS = 1e-05
+MESH = pl.DeviceIdType.MESH
 
 def tile(ref, base, lanes):
     return ref[pl.ds(pl.multiple_of(base, UNROLL), UNROLL), lanes]
@@ -278,6 +279,236 @@
     return result
 
 
+def bit_positions(sizes):
+    return [(axis, size.bit_length() - 2 - k) for axis, size in sizes for k in range(size.bit_length() - 1)]
+
+
+def own_bit(place):
+    axis, level = place
+    return lax.rem(lax.axis_index(axis) // 2**level, 2)
+
+
+def partner(place):
+    axis, level = place
+    where = {"ctx": lax.axis_index("ctx"), "exp": lax.axis_index("exp")}
+    where[axis] = where[axis] + (1 - 2 * own_bit(place)) * 2**level
+    return (where["ctx"], where["exp"])
+
+
+def meet(places):
+    barrier = pltpu.get_barrier_semaphore()
+    for place in places:
+        pl.semaphore_signal(barrier, inc=1, device_id=partner(place), device_id_type=MESH)
+    pl.semaphore_wait(barrier, len(places))
+
+
+def gather_kernel(places, streams, count, *refs):
+    shards, wholes = refs[:count], refs[count : 2 * count]
+    send_sems, recv_sems, local_sems = refs[2 * count :]
+    bits = [own_bit(place) for place in places]
+
+    def view(stream, have):
+        array, cols, order = stream
+        index = tuple(slice(None) if p in have else bits[p] for p in range(len(places)))
+        return wholes[array].at[index + (slice(None), cols)]
+
+    meet(places)
+    locals_ = []
+    for number, stream in enumerate(streams):
+        array, cols, order = stream
+        copy = pltpu.make_async_copy(shards[array].at[:, cols], view(stream, ()), local_sems.at[number])
+        copy.start()
+        locals_.append(copy)
+
+    def send(number, stage):
+        stream = streams[number]
+        array, cols, order = stream
+        source = shards[array].at[:, cols] if stage == 0 else view(stream, order[:stage])
+        copy = pltpu.make_async_remote_copy(
+            src_ref=source,
+            dst_ref=view(stream, order[:stage]),
+            send_sem=send_sems.at[number, stage],
+            recv_sem=recv_sems.at[number, stage],
+            device_id=partner(places[order[stage]]),
+            device_id_type=MESH,
+        )
+        copy.start()
+        return copy
+
+    stages = len(places)
+    flights = [[send(number, 0)] for number in range(len(streams))]
+    for copy in locals_:
+        copy.wait()
+    for stage in range(stages):
+        for number in range(len(streams)):
+            flights[number][stage].wait_recv()
+            if stage + 1 < stages:
+                flights[number].append(send(number, stage + 1))
+    for flight in flights:
+        for copy in flight:
+            copy.wait_send()
+
+
+def orders_of(places):
+    core = places.index(("ctx", 0))
+    rows = [k for k, place in enumerate(places) if place[0] == "ctx" and place[1] > 0]
+    near = places.index(("exp", 0))
+    far = [k for k, place in sorted(enumerate(places), key=lambda item: item[1][1]) if place[0] == "exp" and place[1] > 0]
+    return [core] + rows + [near] + far, [core, near] + rows + far
+
+
+def gather_all(sizes, shards, identity):
+    places = bit_positions(sizes)
+    first, second = [tuple(reversed(order)) for order in orders_of(places)]
+    streams = []
+    for array, shard in enumerate(shards):
+        width = shard.shape[1]
+        if width % 256 == 0:
+            streams.append((array, slice(0, width // 2), first))
+            streams.append((array, slice(width // 2, width), second))
+        else:
+            streams.append((array, slice(0, width), first if array % 2 else second))
+    stages = len(places)
+    anywhere = pl.BlockSpec(memory_space=pl.ANY)
+    wholes = pl.pallas_call(
+        functools.partial(gather_kernel, places, streams, len(shards)),
+        in_specs=[anywhere] * len(shards),
+        out_specs=[anywhere] * len(shards),
+        out_shape=[jax.ShapeDtypeStruct((2,) * stages + shard.shape, shard.dtype) for shard in shards],
+        scratch_shapes=[
+            pltpu.SemaphoreType.DMA((len(streams), stages)),
+            pltpu.SemaphoreType.DMA((len(streams), stages)),
+            pltpu.SemaphoreType.DMA((len(streams),)),
+        ],
+        compiler_params=pltpu.CompilerParams(collective_id=identity, has_side_effects=True),
+        name="gather_all",
+    )(*shards)
+    return [whole.reshape((-1,) + whole.shape[stages + 1 :]) for whole in wholes]
+
+
+def reduce_kernel(places, streams, count, *refs):
+    parts, totals = refs[:count], refs[count : 2 * count]
+    stages = len(places)
+    landing = refs[2 * count : 2 * count + len(streams) * stages]
+    send_sems, recv_sems = refs[2 * count + len(streams) * stages :]
+    bits = [own_bit(place) for place in places]
+
+    def spot(number, stage):
+        return landing[number * stages + stage]
+
+    def side(number, stage, value):
+        array, cols, order = streams[number]
+        left = [p for p in range(stages) if p not in order[:stage]]
+        index = tuple(value if p == order[stage] else slice(None) for p in left)
+        if stage == 0:
+            return parts[array].at[index + (slice(None), cols)]
+        return spot(number, stage - 1).at[index]
+
+    meet(places)
+
+    def send(number, stage):
+        order = streams[number][2]
+        copy = pltpu.make_async_remote_copy(
+            src_ref=side(number, stage, 1 - bits[order[stage]]),
+            dst_ref=spot(number, stage),
+            send_sem=send_sems.at[number, stage],
+            recv_sem=recv_sems.at[number, stage],
+            device_id=partner(places[order[stage]]),
+            device_id_type=MESH,
+        )
+        copy.start()
+        return copy
+
+    flights = [[send(number, 0)] for number in range(len(streams))]
+    for stage in range(stages):
+        for number, (array, cols, order) in enumerate(streams):
+            flights[number][stage].wait_recv()
+            mine = side(number, stage, bits[order[stage]])
+            there = spot(number, stage)
+            if stage + 1 < stages:
+                depth = stages - stage - 1
+
+                def add(index, unused):
+                    at = tuple(lax.rem(index // 2 ** (depth - 1 - k), 2) for k in range(depth))
+                    there[at] = (there[at].astype(jnp.float32) + mine[at].astype(jnp.float32)).astype(there.dtype)
+                    return unused
+
+                lax.fori_loop(0, 2**depth, add, 0)
+                flights[number].append(send(number, stage + 1))
+            else:
+                totals[array][:, cols] = there[...].astype(jnp.float32) + mine[...].astype(jnp.float32)
+    for flight in flights:
+        for copy in flight:
+            copy.wait_send()
+
+
+def reduce_all(sizes, parts, identity):
+    places = bit_positions(sizes)
+    first, second = [tuple(order) for order in orders_of(places)]
+    stages = len(places)
+    streams = []
+    blocks = []
+    for array, part in enumerate(parts):
+        width = part.shape[1]
+        blocks.append(part.reshape((2,) * stages + (-1, width)))
+        if width % 256 == 0:
+            streams.append((array, slice(0, width // 2), first))
+            streams.append((array, slice(width // 2, width), second))
+        else:
+            streams.append((array, slice(0, width), first if array % 2 else second))
+    inside = pl.BlockSpec(memory_space=pltpu.VMEM)
+    landing = []
+    for array, cols, order in streams:
+        for stage in range(stages):
+            rows = blocks[array].shape[-2]
+            landing.append(pltpu.VMEM((2,) * (stages - stage - 1) + (rows, cols.stop - cols.start), jnp.bfloat16))
+    return pl.pallas_call(
+        functools.partial(reduce_kernel, places, streams, len(parts)),
+        in_specs=[inside] * len(parts),
+        out_specs=[inside] * len(parts),
+        out_shape=[jax.ShapeDtypeStruct(block.shape[-2:], jnp.float32) for block in blocks],
+        scratch_shapes=landing
+        + [
+            pltpu.SemaphoreType.DMA((len(streams), stages)),
+            pltpu.SemaphoreType.DMA((len(streams), stages)),
+        ],
+        compiler_params=pltpu.CompilerParams(
+            collective_id=identity, has_side_effects=True, vmem_limit_bytes=48 * 1024 * 1024
+        ),
+        name="reduce_all",
+    )(*blocks)
+
+
+def dot(left, right):
+    return jnp.dot(left, right, preferred_element_type=jnp.float32)
+
+
+def flipped(value, level):
+    count = lax.axis_size("ctx")
+    return lax.ppermute(value, "ctx", [(source, source ^ (1 << level)) for source in range(count)])
+
+
+def spread_slices(own):
+    levels = lax.axis_size("ctx").bit_length() - 1
+    slices = {0: own}
+    for level in reversed(range(levels)):
+        for offset in sorted(slices):
+            slices[offset + (1 << level)] = flipped(slices[offset], level)
+    return [slices[offset] for offset in sorted(slices)]
+
+
+def collect_slices(sums):
+    levels = lax.axis_size("ctx").bit_length() - 1
+    for level in range(levels):
+        step = 1 << level
+        kept = {}
+        for offset in range(0, len(sums), 2 * step):
+            arrived = flipped(sums[offset + step].astype(jnp.bfloat16), level)
+            kept[offset] = sums[offset] + arrived.astype(jnp.float32)
+        sums = [kept.get(offset) for offset in range(len(sums))]
+    return sums[0]
+
+
 def body(
     inputs,
     segments,
@@ -298,7 +529,6 @@
     expert_in,
     expert_out,
 ):
-    everyone = ("ctx", "exp")
     experts = router.shape[1]
     half_rows = norm_gain.shape[0]
     columns = (
@@ -314,9 +544,10 @@
     )
     widths = [part.shape[1] for part in columns]
     ends = [sum(widths[: k + 1]) for k in range(len(widths))]
-    full_small = lax.all_gather(jnp.concatenate(columns, axis=1), everyone, axis=0, tiled=True)
-    full_in = lax.all_gather(in_proj, everyone, axis=0, tiled=True)
-    full_out = lax.all_gather(out_proj, everyone, axis=0, tiled=True)
+    sizes = [(name, lax.axis_size(name)) for name in ("ctx", "exp")]
+    full_in, full_out, full_small = gather_all(
+        sizes, (in_proj, out_proj, jnp.concatenate(columns, axis=1)), 0
+    )
     full_xproj, full_dt, full_taps, full_bias, full_dtbias, full_decay, full_skip, gains, full_router = [
         full_small[:, end - width : end] for end, width in zip(ends, widths)
     ]
@@ -412,19 +643,14 @@
         .set(normed_two)
         .reshape(experts, capacity, D)
     )
-    full_expert_in, full_expert_out = (
-        lax.all_gather(expert_in, "ctx", axis=2, tiled=True),
-        lax.all_gather(expert_out, "ctx", axis=1, tiled=True),
-    )
-    weight_in = full_expert_in[0]
-    weight_out = full_expert_out[0]
+    weights_in = spread_slices(expert_in[0])
+    weights_out = spread_slices(expert_out[0])
     rows_in = lax.all_to_all(buffer, "exp", split_axis=0, concat_axis=0, tiled=True)
-    hidden_pre = jnp.einsum("srd,df->srf", rows_in, weight_in, preferred_element_type=jnp.float32)
-    active = jax.nn.gelu(hidden_pre, approximate=False).astype(jnp.bfloat16)
-    result = jnp.einsum(
-        "srf,fd->srd", active, weight_out, preferred_element_type=jnp.float32
-    ).astype(jnp.bfloat16)
-    expert_result, hidden_pre, active, received = (result, hidden_pre, active, rows_in)
+    rows_in = rows_in.reshape(experts * capacity, D)
+    hidden_pre = [dot(rows_in, weight) for weight in weights_in]
+    active = [jax.nn.gelu(values, approximate=False).astype(jnp.bfloat16) for values in hidden_pre]
+    result = sum(dot(values, weight) for values, weight in zip(active, weights_out)).astype(jnp.bfloat16)
+    expert_result = result.reshape(experts, capacity, D)
     returned = lax.all_to_all(expert_result, "exp", split_axis=0, concat_axis=0, tiled=True)
     picked = returned.reshape(-1, D)[target].astype(jnp.float32)
     outcome = residual + gate_val[:, None] * picked
@@ -439,32 +665,19 @@
         .reshape(experts, capacity, D)
     )
     grad_result = lax.all_to_all(grad_buffer, "exp", split_axis=0, concat_axis=0, tiled=True)
-    grad_active = jnp.einsum(
-        "srd,fd->srf", grad_result, weight_out, preferred_element_type=jnp.float32
-    )
-    grad_expert_out = jnp.einsum(
-        "srf,srd->fd", active, grad_result, preferred_element_type=jnp.float32
-    )
-    gelu_value, gelu_pull = jax.vjp(
-        lambda values: jax.nn.gelu(values, approximate=False), hidden_pre
-    )
-    grad_hidden = gelu_pull(grad_active)[0].astype(jnp.bfloat16)
-    grad_expert_in = jnp.einsum(
-        "srd,srf->df", received, grad_hidden, preferred_element_type=jnp.float32
-    )
-    grad_rows = jnp.einsum(
-        "srf,df->srd", grad_hidden, weight_in, preferred_element_type=jnp.float32
-    ).astype(jnp.bfloat16)
+    grad_result = grad_result.reshape(experts * capacity, D)
+    grad_expert_out = [dot(values.T, grad_result) for values in active]
+    grad_hidden = []
+    for values, weight in zip(hidden_pre, weights_out):
+        gelu_value, gelu_pull = jax.vjp(lambda inner: jax.nn.gelu(inner, approximate=False), values)
+        grad_hidden.append(gelu_pull(dot(grad_result, weight.T))[0].astype(jnp.bfloat16))
+    grad_expert_in = [dot(rows_in.T, values) for values in grad_hidden]
+    grad_rows = sum(dot(values, weight.T) for values, weight in zip(grad_hidden, weights_in))
+    grad_rows = grad_rows.astype(jnp.bfloat16).reshape(experts, capacity, D)
     grad_sent = lax.all_to_all(grad_rows, "exp", split_axis=0, concat_axis=0, tiled=True)
     grad_from_experts = grad_sent.reshape(-1, D)[target].astype(jnp.float32)
-    grad_w_in, grad_w_out = (
-        lax.psum_scatter(
-            grad_expert_in[None].astype(jnp.bfloat16), "ctx", scatter_dimension=2, tiled=True
-        ).astype(jnp.float32),
-        lax.psum_scatter(
-            grad_expert_out[None].astype(jnp.bfloat16), "ctx", scatter_dimension=1, tiled=True
-        ).astype(jnp.float32),
-    )
+    grad_w_in = collect_slices(grad_expert_in)[None]
+    grad_w_out = collect_slices(grad_expert_out)[None]
     grad_probs = grad_gate[:, None] * one_float
     grad_logits = (
         probability * (grad_probs - jnp.sum(grad_probs * probability, axis=1, keepdims=True))
@@ -543,12 +756,15 @@
         grad_router.reshape(-1, experts // 2),
     )
 
-    def scatter(values):
-        return lax.psum_scatter(values, everyone, scatter_dimension=0, tiled=True)
-
-    own_in = scatter(grad_in_proj.astype(jnp.bfloat16)).astype(jnp.float32)
-    own_out = scatter(grad_out_proj.astype(jnp.bfloat16)).astype(jnp.float32)
-    own_small = scatter(jnp.concatenate(sums, axis=1))
+    own_in, own_out, own_small = reduce_all(
+        sizes,
+        (
+            grad_in_proj.astype(jnp.bfloat16),
+            grad_out_proj.astype(jnp.bfloat16),
+            jnp.concatenate(sums, axis=1).astype(jnp.bfloat16),
+        ),
+        1,
+    )
     own_x, own_dt, own_taps, own_bias, own_dtbias, own_decay, own_skip, own_gains, own_router = [
         own_small[:, end - width : end] for end, width in zip(ends, widths)
     ]

time: 855 us -> 595 us (0.70)
  the two profiles are of different devices: /device:TPU:0 before, /device:TPU:8 now
where the time goes in v2:
time: 595 us; the launch traced here: 584 us
  Pallas kernels  191 us (32%)
  matrix products  115 us (19%)
  waiting for transfers between devices  86.1 us (14%)
  local copies, waits for them, and re-layouts  69.3 us (12%)
  other arithmetic  49.1 us (8%)
  starting transfers between devices  36.4 us (6%)
  blocking collectives  35 us (6%)
    dot_general x24, matrix products, dot(): return jnp.dot(left, right, preferred_element_type=jnp.float32)  76.5 us
    pallas_call x1, Pallas kernels, reduce_all(): pl.pallas_call(functools.partial(reduce_kernel, places, streams, len(part...  64 us
    pallas_call x1, Pallas kernels, gather_all(): pl.pallas_call(functools.partial(gather_kernel, places, streams, len(shar...  56.5 us
    ppermute x12, waiting for transfers between devices, flipped(): lax.ppermute(value, 'ctx', [(source, source ^ 1 << level) for source in r...  51 us
    pallas_call x1, Pallas kernels, scan_adjoint(): pl.pallas_call(functools.partial(adjoint_kernel, pick(channels)), grid=(t...  35 us
    all_gather x1, blocking collectives, body(): lax.all_gather(local_inflow[None].astype(jnp.bfloat16), 'ctx', axis=0, ti...  27 us
    unnamed x219, local copies, waits for them, and re-layouts  23.7 us
    pallas_call x1, Pallas kernels, scan_out(): pl.pallas_call(functools.partial(out_kernel, pick(channels)), grid=(token...  18.1 us
  transfers between devices with their start and end apart: 19, of which 5 were waited for; matrix products, arithmetic and copies ran while one was open for 26% of the time, Pallas kernels for 28%

profile of v2, /device:TPU:8, one launch (start us, length us, event | category | flops | bytes accessed | tf_op | source)
XLA Modules:
  0.0 584.2 jit_solution(3587320370155945345)
XLA Ops:
  10.9 56.5 %gather_all.1 = (bf16[2,2,2,2,2,24,3072]{6,5,4,3,2,1,0:T(8,128)(2,1)}, bf16[2,2,2,2,2,48,768]{6,5,4,3,2,1,0:T(8,128)(2,1)}, bf16[2,2,2,2,2,48,156]{6,5,4,3,2,1,0:T(8,128)(2,1)}) custom-call(bf16[24,3072]{1,0:T(8,128)(2,1)} %refs_0_.1, bf16[48,768]{1,0:T(8,128)(2,1)} %refs_1_.1, bf16[48,156]{1,0:T(8,128)(2,1)} %concatenate.66.refs_2_), custom_call_target="tpu_custom_call" | custom-call | tf_op jit(solution)/shard_map/gather_all/pallas_call | solution.py:373
  70.3 6.6 %fusion.145 = (bf16[384,3072]{1,0:T(8,128)(2,1)S(1)}, f32[384,3072]{1,0:T(8,128)}) fusion(bf16[768,3072]{1,0:T(8,128)(2,1)} %bitcast.253, bf16[1,384,768]{2,1,0:T(8,128)(2,1)S(1)} %copy-done.34, f32[768]{0:T(1024)S(1)} %reshape.383, f32[384]{0:T(512)S(1)} %fusion.112), kind=kOutput, calls=%fused_computation.301 | convolution fusion | flops 1814298624 | bytes 12390912 | tf_op jit(solution)/shard_map/dot_general | solution.py:566
  77.0 2.4 collective-permute-start.1
  80.7 2.7 slice_reduce_fusion.3
  88.8 3.2 multiply_convert_fusion.1
  94.1 4.4 fusion.141
  98.6 2.4 broadcast_in_dim.57.b_ref
  101.0 8.5 %shard_map.297 = f32[16,1536]{1,0:T(8,128)S(1)} custom-call(f32[384,1536]{1,0:T(8,128)S(1)} %get-tuple-element.146.step_ref, f32[384,1536]{1,0:T(8,128)S(1)} %get-tuple-element.154.push_ref, f32[384,16,128]{2,1,0:T(8,128)} %broadcast_in_dim.57.b_ref, f32[16,1536]{1,0:T(8,128)S(1)} %get-tuple-element.164.rate_ref), custom_call_target="tpu_custom_call" | custom-call | tf_op jit(solution)/shard_map/pallas_call | solution.py:199
  110.9 8.1 %all_gather.6 = bf16[4,2,16,1536]{3,2,1,0:T(8,128)(2,1)S(1)} all-gather(bf16[1,2,16,1536]{3,2,1,0:T(8,128)(2,1)S(1)} %pad_maximum_fusion.3), channel_id=1, replica_groups=mesh['ctx'=4,'exp'=8] {'ctx'}, dimensions={0}, use_global_device_ids=true | all-gather | bytes 491520 | tf_op jit(solution)/shard_map/all_gather | solution.py:604
  122.1 18.1 %shard_map.298 = (f32[384,1536]{1,0:T(8,128)S(1)}, bf16[384,16,1536]{2,1,0:T(8,128)(2,1)}, bf16[6,16,1536]{2,1,0:T(8,128)(2,1)S(1)}) custom-call(f32[384,1536]{1,0:T(8,128)S(1)} %get-tuple-element.146.step_ref, f32[384,1536]{1,0:T(8,128)} %copy-done.1, f32[384,16,128]{2,1,0:T(8,128)} %broadcast_in_dim.57.b_ref, f32[384,16,128]{2,1,0:T(8,128)} %broadcast_in_dim.58.c_ref, ...), custom_call_target="tpu_custom_call" | custom-call | tf_op jit(solution)/shard_map/pallas_call | solution.py:214
  145.4 3.1 scatter_custom_fusion
  149.6 6.6 %all-to-all-start = ((bf16[8,60,768]{2,1,0:T(8,128)(2,1)}), bf16[8,60,768]{2,1,0:T(8,128)(2,1)S(1)}, u32[]{:S(2)}, u32[]{:S(2)}) async-start(bf16[8,60,768]{2,1,0:T(8,128)(2,1)} %reshape.370), calls=%async_computation | async-start | bytes 1572864 | tf_op jit(solution)/shard_map/all_to_all | solution.py:648
  158.7 26.6 %collective-permute-done.4 = bf16[768,768]{1,0:T(8,128)(2,1)} collective-permute-done((bf16[768,768]{1,0:T(8,128)(2,1)}, bf16[768,768]{1,0:T(8,128)(2,1)}, u32[]{:S(2)}, u32[]{:S(2)}) %collective-permute-start.4) | collective-permute-done | bytes 1179680 | tf_op jit(solution)/shard_map/ppermute | solution.py:488
  185.3 24.4 %collective-permute-done.5 = bf16[768,768]{1,0:T(8,128)(2,1)} collective-permute-done((bf16[768,768]{1,0:T(8,128)(2,1)}, bf16[768,768]{1,0:T(8,128)(2,1)}, u32[]{:S(2)}, u32[]{:S(2)}) %collective-permute-start.5) | collective-permute-done | bytes 1179680 | tf_op jit(solution)/shard_map/ppermute | solution.py:488
  210.7 6.7 %multiply_convert_fusion.5 = (bf16[480,768]{1,0:T(8,128)(2,1)S(1)}, f32[480,768]{1,0:T(8,128)}, f32[480,768]{1,0:T(8,128)}) fusion(bf16[480,768]{1,0:T(8,128)(2,1)} %reshape.371, bf16[1,768,768]{2,1,0:T(8,128)(2,1)} %param.34), kind=kOutput, calls=%fused_computation.118 | convolution fusion | flops 590192640 | bytes 5603328 | tf_op jit(solution)/shard_map/dot_general | solution.py:483
  218.8 6.0 %multiply_convert_fusion.3 = (bf16[480,768]{1,0:T(8,128)(2,1)S(1)}, f32[480,768]{1,0:T(8,128)}, f32[480,768]{1,0:T(8,128)}) fusion(bf16[480,768]{1,0:T(8,128)(2,1)S(1)} %copy-done.29, bf16[768,768]{1,0:T(8,128)(2,1)} %collective-permute-done.4), kind=kOutput, calls=%fused_computation.92 | convolution fusion | flops 590192640 | bytes 5603328 | tf_op jit(solution)/shard_map/dot_general | solution.py:483
  227.1 6.0 %multiply_convert_fusion.4 = (bf16[480,768]{1,0:T(8,128)(2,1)S(1)}, f32[480,768]{1,0:T(8,128)}, f32[480,768]{1,0:T(8,128)}) fusion(bf16[480,768]{1,0:T(8,128)(2,1)S(1)} %copy-done.29, bf16[768,768]{1,0:T(8,128)(2,1)} %collective-permute-done.2), kind=kOutput, calls=%fused_computation.105 | convolution fusion | flops 590192640 | bytes 5603328 | tf_op jit(solution)/shard_map/dot_general | solution.py:483
  235.5 15.3 %multiply_convert_fusion.2 = (bf16[480,768]{1,0:T(8,128)(2,1)S(1)}, f32[480,768]{1,0:T(8,128)}, f32[480,768]{1,0:T(8,128)}) fusion(bf16[480,768]{1,0:T(8,128)(2,1)S(1)} %copy-done.29, bf16[768,768]{1,0:T(8,128)(2,1)} %collective-permute-done.6), kind=kOutput, calls=%fused_computation.79 | convolution fusion | flops 590192640 | bytes 5603328 | tf_op jit(solution)/shard_map/dot_general | solution.py:483
  254.8 6.2 %all-to-all-start.1 = ((bf16[8,60,768]{2,1,0:T(8,128)(2,1)}), bf16[8,60,768]{2,1,0:T(8,128)(2,1)}, u32[]{:S(2)}, u32[]{:S(2)}) async-start(bf16[8,60,768]{2,1,0:T(8,128)(2,1)} %reshape.372), calls=%async_computation.1 | async-start | bytes 1572864 | tf_op jit(solution)/shard_map/all_to_all | solution.py:654
  264.0 16.0 %all-to-all-done.1 = bf16[8,60,768]{2,1,0:T(8,128)(2,1)} async-done(((bf16[8,60,768]{2,1,0:T(8,128)(2,1)}), bf16[8,60,768]{2,1,0:T(8,128)(2,1)}, u32[]{:S(2)}, u32[]{:S(2)}) %all-to-all-start.1) | async-done | bytes 737312 | tf_op jit(solution)/shard_map/all_to_all | solution.py:654
  281.2 2.6 gather_fusion
  285.4 3.1 scatter_custom_fusion.1
  290.7 6.1 %all-to-all-start.2 = ((bf16[8,60,768]{2,1,0:T(8,128)(2,1)}), bf16[8,60,768]{2,1,0:T(8,128)(2,1)}, u32[]{:S(2)}, u32[]{:S(2)}) async-start(bf16[8,60,768]{2,1,0:T(8,128)(2,1)} %reshape.374), calls=%async_computation.2 | async-start | bytes 1572864 | tf_op jit(solution)/shard_map/all_to_all | solution.py:667
  298.1 17.1 %all-to-all-done.2 = bf16[8,60,768]{2,1,0:T(8,128)(2,1)} async-done(((bf16[8,60,768]{2,1,0:T(8,128)(2,1)}), bf16[8,60,768]{2,1,0:T(8,128)(2,1)}, u32[]{:S(2)}, u32[]{:S(2)}) %all-to-all-start.2) | async-done | bytes 737312 | tf_op jit(solution)/shard_map/all_to_all | solution.py:667
  316.5 3.3 convolution_convert_fusion.4
  319.8 2.5 add_convert_fusion.6
  324.4 2.4 add_convert_fusion.3
  331.1 2.3 fusion.150
  333.5 2.3 add_convert_fusion.5
  341.3 6.3 %all-to-all-start.3 = ((bf16[8,60,768]{2,1,0:T(8,128)(2,1)}), bf16[8,60,768]{2,1,0:T(8,128)(2,1)}, u32[]{:S(2)}, u32[]{:S(2)}) async-start(bf16[8,60,768]{2,1,0:T(8,128)(2,1)} %reshape.376), calls=%async_computation.3 | async-start | bytes 1572864 | tf_op jit(solution)/shard_map/all_to_all | solution.py:677
  348.2 2.9 convolution_convert_fusion.7
  367.0 2.7 gather_fusion.1
  374.3 4.8 fusion.8
  379.1 9.1 %shard_map.299 = f32[16,1536]{1,0:T(8,128)S(1)} custom-call(f32[384,1536]{1,0:T(8,128)S(1)} %get-tuple-element.146.step_ref, f32[384,1536]{1,0:T(8,128)S(1)} %get-tuple-element.134.grad_ref, f32[384,16,128]{2,1,0:T(8,128)} %broadcast_in_dim.58.c_ref, f32[16,1536]{1,0:T(8,128)S(1)} %get-tuple-element.164.rate_ref), custom_call_target="tpu_custom_call" | custom-call | tf_op jit(solution)/shard_map/pallas_call | solution.py:229
  388.2 27.0 %all-gather = bf16[64,1536]{1,0:T(8,128)(2,1)S(1)} all-gather(bf16[16,1536]{1,0:T(8,128)(2,1)S(1)} %convert_element_type.291), channel_id=2, replica_groups=mesh['ctx'=4,'exp'=8] {'ctx'}, dimensions={0}, use_global_device_ids=true | all-gather | bytes 245760 | tf_op jit(solution)/shard_map/all_gather | solution.py:697
  415.3 35.0 %shard_map.300 = (f32[384,1536]{1,0:T(8,128)S(1)}, f32[384,1536]{1,0:T(8,128)S(1)}, f32[384,16,128]{2,1,0:T(8,128)}, f32[384,16,128]{2,1,0:T(8,128)}, f32[16,1536]{1,0:T(8,128)S(1)}) custom-call(f32[384,1536]{1,0:T(8,128)} %copy-done, f32[384,1536]{1,0:T(8,128)} %copy-done.1, f32[384,1536]{1,0:T(8,128)} %copy-done.2, ...), custom_call_target="tpu_custom_call" | custom-call | tf_op jit(solution)/shard_map/pallas_call | solution.py:245
  451.7 2.8 reduce_sum.202
  454.5 2.8 reduce_sum.198
  457.5 3.7 fusion.135
  463.3 4.5 multiply_reduce_fusion.3
  467.7 2.6 pad_add_fusion
  486.6 5.5 fusion.44
  492.1 4.6 convolution_convert_fusion
  497.9 4.5 concatenate.81.refs_2_
  502.5 64.0 %reduce_all.1 = (f32[24,3072]{1,0:T(8,128)S(1)}, f32[48,768]{1,0:T(8,128)S(1)}, f32[48,156]{1,0:T(8,128)S(1)}) custom-call(bf16[2,2,2,2,2,24,3072]{6,5,4,3,2,1,0:T(8,128)(2,1)} %bitcast.240, bf16[2,2,2,2,2,48,768]{6,5,4,3,2,1,0:T(8,128)(2,1)S(1)} %bitcast.231, bf16[2,2,2,2,2,48,156]{6,5,4,3,2,1,0:T(8,128)(2,1)S(1)} %concatenate.81.refs_2_), custom_call_target="tpu_custom_call" | custom-call | tf_op jit(solution)/shard_map/reduce_all/pallas_call | solution.py:465
  572.2 3.3 fusion.52
  575.5 3.6 add_bitcast_fusion.1
  579.1 3.5 add_bitcast_fusion
  (369 shorter events, 117.4 us)
Async XLA Ops:
  0.6 69.6 %copy-start.34 = (bf16[1,384,768]{2,1,0:T(8,128)(2,1)S(1)}, bf16[1,384,768]{2,1,0:T(8,128)(2,1)}, u32[]{:S(2)}) copy-start(bf16[1,384,768]{2,1,0:T(8,128)(2,1)} %param.18) | copy-start | bytes 1769476
  1.4 84.7 %collective-permute-start = (bf16[3]{0:T(256)(128)(2,1)S(1)}, bf16[3]{0:T(256)(128)(2,1)S(1)}, u32[]{:S(2)}, u32[]{:S(2)}) collective-permute-start(bf16[3]{0:T(256)(128)(2,1)S(1)} %fusion.115), channel_id=1, source_target_pairs={{0,8},{8,16},{16,24},{1,9},{9,17},{17,25},{2,10},{10,18},{18,26},{... | collective-permute-start | bytes 26 | tf_op jit(solution)/shard_map/ppermute | solution.py:262
  69.0 7.9 %copy-start.68 = (f32[768]{0:T(1024)}, f32[768]{0:T(1024)S(1)}, u32[]{:S(2)}) copy-start(f32[768]{0:T(1024)S(1)} %reshape.383) | copy-start | bytes 9220
  70.3 6.7 %copy-start.66 = (f32[384]{0:T(512)}, f32[384]{0:T(512)S(1)}, u32[]{:S(2)}) copy-start(f32[384]{0:T(512)S(1)} %fusion.47) | copy-start | bytes 4612
  70.3 6.7 %copy-start.77 = (f32[384]{0:T(512)}, f32[384]{0:T(512)S(1)}, u32[]{:S(2)}) copy-start(f32[384]{0:T(512)S(1)} %fusion.112) | copy-start | bytes 4612
  70.3 9.1 %copy-start.80 = (s32[1,384]{1,0:T(1,128)S(1)}, s32[1,384]{1,0:T(1,128)}, u32[]{:S(2)}) copy-start(s32[1,384]{1,0:T(1,128)} %param.19) | copy-start | bytes 4612
  77.0 11.1 %collective-permute-start.1 = (bf16[3,1536]{1,0:T(4,128)(2,1)S(1)}, bf16[3,1536]{1,0:T(4,128)(2,1)S(1)}, u32[]{:S(2)}, u32[]{:S(2)}) collective-permute-start(bf16[3,1536]{1,0:T(4,128)(2,1)S(1)} %slice.273), channel_id=1, source_target_pairs={{0,8},{8,16},{16,24},{1,9},{9,17},{17,25},{2,10},{10,18},{18,26},{... | collective-permute-start | bytes 27656 | tf_op jit(solution)/shard_map/ppermute | solution.py:262
  83.4 5.0 copy-start.55
  92.0 6.6 %copy-start.11 = (bf16[384,1536]{1,0:T(8,128)(2,1)}, bf16[384,1536]{1,0:T(8,128)(2,1)S(1)}, u32[]{:S(2)}) copy-start(bf16[384,1536]{1,0:T(8,128)(2,1)S(1)} %get-tuple-element.147) | copy-start | bytes 3538948
  94.1 4.5 copy-start.45
  98.5 280.6 %copy-start = (f32[384,1536]{1,0:T(8,128)}, f32[384,1536]{1,0:T(8,128)S(1)}, u32[]{:S(2)}) copy-start(f32[384,1536]{1,0:T(8,128)S(1)} %get-tuple-element.146.step_ref) | copy-start | bytes 7077892
  110.9 9.1 %copy-start.44 = (f32[384,16]{1,0:T(8,128)S(1)}, f32[384,16]{1,0:T(8,128)}, u32[]{:S(2)}) copy-start(f32[384,16]{1,0:T(8,128)} %copy.112) | copy-start | bytes 73732
  120.0 20.2 %slice-start = ((s8[4718592]{0:T(1024)(128)(4,1)}), s8[4194304]{0:T(1024)(128)(4,1)S(1)}, s32[]{:S(2)}) async-start(s8[4718592]{0:T(1024)(128)(4,1)} %bitcast.245), calls=%async_computation.4 | async-start | bytes 8388608
  122.1 18.1 %copy-start.12 = (bf16[384,1536]{1,0:T(8,128)(2,1)S(1)}, bf16[384,1536]{1,0:T(8,128)(2,1)}, u32[]{:S(2)}) copy-start(bf16[384,1536]{1,0:T(8,128)(2,1)} %copy-done.11) | copy-start | bytes 3538948
  122.1 18.1 %slice-start.1 = ((s8[4718592]{0:T(1024)(128)(4,1)}), s8[524288]{0:T(1024)(128)(4,1)S(1)}, s32[]{:S(2)}) async-start(s8[4718592]{0:T(1024)(128)(4,1)} %bitcast.245), calls=%async_computation.5 | async-start | bytes 1048576
  122.1 18.1 %copy-start.63 = (f32[1536]{0:T(1024)S(1)}, f32[1536]{0:T(1024)}, u32[]{:S(2)}) copy-start(f32[1536]{0:T(1024)} %get-tuple-element.184) | copy-start | bytes 18436
  149.6 60.1 %all-to-all-start = ((bf16[8,60,768]{2,1,0:T(8,128)(2,1)}), bf16[8,60,768]{2,1,0:T(8,128)(2,1)S(1)}, u32[]{:S(2)}, u32[]{:S(2)}) async-start(bf16[8,60,768]{2,1,0:T(8,128)(2,1)} %reshape.370), calls=%async_computation | async-start | bytes 1572864 | tf_op jit(solution)/shard_map/all_to_all | solution.py:648
  156.2 29.1 %collective-permute-start.4 = (bf16[768,768]{1,0:T(8,128)(2,1)}, bf16[768,768]{1,0:T(8,128)(2,1)}, u32[]{:S(2)}, u32[]{:S(2)}) collective-permute-start(bf16[768,768]{1,0:T(8,128)(2,1)} %bitcast.259), channel_id=1, source_target_pairs={{0,16},{8,24},{16,0},{24,8},{1,17},{9,25},{17,1},{25,9},{2,18},{10... | collective-permute-start | bytes 3538952 | tf_op jit(solution)/shard_map/ppermute | solution.py:488
  157.3 52.5 %collective-permute-start.5 = (bf16[768,768]{1,0:T(8,128)(2,1)}, bf16[768,768]{1,0:T(8,128)(2,1)}, u32[]{:S(2)}, u32[]{:S(2)}) collective-permute-start(bf16[768,768]{1,0:T(8,128)(2,1)} %bitcast.257), channel_id=1, source_target_pairs={{0,16},{8,24},{16,0},{24,8},{1,17},{9,25},{17,1},{25,9},{2,18},{10... | collective-permute-start | bytes 3538952 | tf_op jit(solution)/shard_map/ppermute | solution.py:488
  158.2 68.9 %collective-permute-start.2 = (bf16[768,768]{1,0:T(8,128)(2,1)}, bf16[768,768]{1,0:T(8,128)(2,1)}, u32[]{:S(2)}, u32[]{:S(2)}) collective-permute-start(bf16[768,768]{1,0:T(8,128)(2,1)} %bitcast.260), channel_id=1, source_target_pairs={{0,8},{8,0},{16,24},{24,16},{1,9},{9,1},{17,25},{25,17},{2,10},{10... | collective-permute-start | bytes 3538952 | tf_op jit(solution)/shard_map/ppermute | solution.py:488
  158.2 74.9 %collective-permute-start.3 = (bf16[768,768]{1,0:T(8,128)(2,1)}, bf16[768,768]{1,0:T(8,128)(2,1)}, u32[]{:S(2)}, u32[]{:S(2)}) collective-permute-start(bf16[768,768]{1,0:T(8,128)(2,1)} %bitcast.258), channel_id=1, source_target_pairs={{0,8},{8,0},{16,24},{24,16},{1,9},{9,1},{17,25},{25,17},{2,10},{10... | collective-permute-start | bytes 3538952 | tf_op jit(solution)/shard_map/ppermute | solution.py:488
  185.3 50.1 %collective-permute-start.6 = (bf16[768,768]{1,0:T(8,128)(2,1)}, bf16[768,768]{1,0:T(8,128)(2,1)}, u32[]{:S(2)}, u32[]{:S(2)}) collective-permute-start(bf16[768,768]{1,0:T(8,128)(2,1)} %collective-permute-done.4), channel_id=1, source_target_pairs={{0,8},{8,0},{16,24},{24,16},{1,9},{9,1},{17,25},{25,17},{2,10},{10... | collective-permute-start | bytes 3538952 | tf_op jit(solution)/shard_map/ppermute | solution.py:488
  209.7 41.1 %collective-permute-start.7 = (bf16[768,768]{1,0:T(8,128)(2,1)}, bf16[768,768]{1,0:T(8,128)(2,1)}, u32[]{:S(2)}, u32[]{:S(2)}) collective-permute-start(bf16[768,768]{1,0:T(8,128)(2,1)} %collective-permute-done.5), channel_id=1, source_target_pairs={{0,8},{8,0},{16,24},{24,16},{1,9},{9,1},{17,25},{25,17},{2,10},{10... | collective-permute-start | bytes 3538952 | tf_op jit(solution)/shard_map/ppermute | solution.py:488
  210.7 6.7 %copy-start.84 = (bf16[1,768,768]{2,1,0:T(8,128)(2,1)S(1)}, bf16[1,768,768]{2,1,0:T(8,128)(2,1)}, u32[]{:S(2)}) copy-start(bf16[1,768,768]{2,1,0:T(8,128)(2,1)} %param.35) | copy-start | bytes 3538948
  253.8 7.4 %copy-start.79 = (s32[384]{0:T(512)S(1)}, s32[384]{0:T(512)}, u32[]{:S(2)}) copy-start(s32[384]{0:T(512)} %fusion.114) | copy-start | bytes 4612
  254.8 6.2 %copy-start.41 = (bf16[1536,4]{1,0:T(8,128)(2,1)S(1)}, bf16[1536,4]{1,0:T(8,128)(2,1)}, u32[]{:S(2)}) copy-start(bf16[1536,4]{1,0:T(8,128)(2,1)} %get-tuple-element.157) | copy-start | bytes 36868
  254.8 25.1 %all-to-all-start.1 = ((bf16[8,60,768]{2,1,0:T(8,128)(2,1)}), bf16[8,60,768]{2,1,0:T(8,128)(2,1)}, u32[]{:S(2)}, u32[]{:S(2)}) async-start(bf16[8,60,768]{2,1,0:T(8,128)(2,1)} %reshape.372), calls=%async_computation.1 | async-start | bytes 1572864 | tf_op jit(solution)/shard_map/all_to_all | solution.py:654
  288.5 8.2 %copy-start.24 = (bf16[384,768]{1,0:T(8,128)(2,1)S(1)}, bf16[384,768]{1,0:T(8,128)(2,1)}, u32[]{:S(2)}) copy-start(bf16[384,768]{1,0:T(8,128)(2,1)} %copy-done.23) | copy-start | bytes 1769476
  290.7 24.6 %all-to-all-start.2 = ((bf16[8,60,768]{2,1,0:T(8,128)(2,1)}), bf16[8,60,768]{2,1,0:T(8,128)(2,1)}, u32[]{:S(2)}, u32[]{:S(2)}) async-start(bf16[8,60,768]{2,1,0:T(8,128)(2,1)} %reshape.374), calls=%async_computation.2 | async-start | bytes 1572864 | tf_op jit(solution)/shard_map/all_to_all | solution.py:667
  316.5 17.0 %copy-start.32 = (bf16[480,768]{1,0:T(8,128)(2,1)}, bf16[480,768]{1,0:T(8,128)(2,1)S(1)}, u32[]{:S(2)}) copy-start(bf16[480,768]{1,0:T(8,128)(2,1)S(1)} %reshape.375) | copy-start | bytes 2211844
  341.3 6.9 %copy-start.31 = (bf16[480,768]{1,0:T(8,128)(2,1)S(1)}, bf16[480,768]{1,0:T(8,128)(2,1)}, u32[]{:S(2)}) copy-start(bf16[480,768]{1,0:T(8,128)(2,1)} %reshape.371) | copy-start | bytes 2211844
  341.3 24.4 %all-to-all-start.3 = ((bf16[8,60,768]{2,1,0:T(8,128)(2,1)}), bf16[8,60,768]{2,1,0:T(8,128)(2,1)}, u32[]{:S(2)}, u32[]{:S(2)}) async-start(bf16[8,60,768]{2,1,0:T(8,128)(2,1)} %reshape.376), calls=%async_computation.3 | async-start | bytes 1572864 | tf_op jit(solution)/shard_map/all_to_all | solution.py:677
  347.6 10.3 %collective-permute-start.10 = (bf16[768,768]{1,0:T(8,128)(2,1)}, bf16[768,768]{1,0:T(8,128)(2,1)S(1)}, u32[]{:S(2)}, u32[]{:S(2)}) collective-permute-start(bf16[768,768]{1,0:T(8,128)(2,1)} %convolution_convert_fusion.6), channel_id=1, source_target_pairs={{0,8},{8,0},{16,24},{24,16},{1,9},{9,1},{17,25},{25,17},{2,10},{10... | collective-permute-start | bytes 3538952 | tf_op jit(solution)/shard_map/ppermute | solution.py:488
  347.7 12.9 %collective-permute-start.13 = (bf16[768,768]{1,0:T(8,128)(2,1)}, bf16[768,768]{1,0:T(8,128)(2,1)S(1)}, u32[]{:S(2)}, u32[]{:S(2)}) collective-permute-start(bf16[768,768]{1,0:T(8,128)(2,1)} %convolution_convert_fusion.4), channel_id=1, source_target_pairs={{0,8},{8,0},{16,24},{24,16},{1,9},{9,1},{17,25},{25,17},{2,10},{10... | collective-permute-start | bytes 3538952 | tf_op jit(solution)/shard_map/ppermute | solution.py:488
  353.1 222.4 %collective-permute-start.9 = (bf16[768,768]{1,0:T(8,128)(2,1)}, bf16[768,768]{1,0:T(8,128)(2,1)}, u32[]{:S(2)}, u32[]{:S(2)}) collective-permute-start(bf16[768,768]{1,0:T(8,128)(2,1)} %convolution_convert_fusion.7), channel_id=1, source_target_pairs={{0,8},{8,0},{16,24},{24,16},{1,9},{9,1},{17,25},{25,17},{2,10},{10... | collective-permute-start | bytes 3538952 | tf_op jit(solution)/shard_map/ppermute | solution.py:488
  353.1 226.0 %collective-permute-start.12 = (bf16[768,768]{1,0:T(8,128)(2,1)}, bf16[768,768]{1,0:T(8,128)(2,1)}, u32[]{:S(2)}, u32[]{:S(2)}) collective-permute-start(bf16[768,768]{1,0:T(8,128)(2,1)} %convolution_convert_fusion.5), channel_id=1, source_target_pairs={{0,8},{8,0},{16,24},{24,16},{1,9},{9,1},{17,25},{25,17},{2,10},{10... | collective-permute-start | bytes 3538952 | tf_op jit(solution)/shard_map/ppermute | solution.py:488
  359.8 215.7 %collective-permute-start.11 = (bf16[768,768]{1,0:T(8,128)(2,1)}, bf16[768,768]{1,0:T(8,128)(2,1)}, u32[]{:S(2)}, u32[]{:S(2)}) collective-permute-start(bf16[768,768]{1,0:T(8,128)(2,1)} %add_convert_fusion.1), channel_id=1, source_target_pairs={{0,16},{8,24},{16,0},{24,8},{1,17},{9,25},{17,1},{25,9},{2,18},{10... | collective-permute-start | bytes 3538952 | tf_op jit(solution)/shard_map/ppermute | solution.py:488
  362.4 216.7 %collective-permute-start.14 = (bf16[768,768]{1,0:T(8,128)(2,1)}, bf16[768,768]{1,0:T(8,128)(2,1)}, u32[]{:S(2)}, u32[]{:S(2)}) collective-permute-start(bf16[768,768]{1,0:T(8,128)(2,1)} %add_convert_fusion), channel_id=1, source_target_pairs={{0,16},{8,24},{16,0},{24,8},{1,17},{9,25},{17,1},{25,9},{2,18},{10... | collective-permute-start | bytes 3538952 | tf_op jit(solution)/shard_map/ppermute | solution.py:488
  373.3 5.8 copy-start.27
  379.1 9.1 %copy-start.2 = (f32[384,1536]{1,0:T(8,128)}, f32[384,1536]{1,0:T(8,128)S(1)}, u32[]{:S(2)}) copy-start(f32[384,1536]{1,0:T(8,128)S(1)} %get-tuple-element.134.grad_ref) | copy-start | bytes 7077892
  379.1 36.1 %copy-start.26 = (f32[4,2,16,1536]{3,2,1,0:T(8,128)S(1)}, f32[4,2,16,1536]{3,2,1,0:T(8,128)}, u32[]{:S(2)}) copy-start(f32[4,2,16,1536]{3,2,1,0:T(8,128)} %copy-done.25) | copy-start | bytes 2359300
  457.4 4.5 copy-start.3
  457.4 4.5 copy-start.10
  457.5 5.1 copy-start.37
  457.5 5.8 copy-start.38
  474.6 9.9 %collective-permute-start.8 = (f32[3,1536]{1,0:T(4,128)S(1)}, f32[3,1536]{1,0:T(4,128)S(1)}, u32[]{:S(2)}, u32[]{:S(2)}) collective-permute-start(f32[3,1536]{1,0:T(4,128)S(1)} %pad_add_fusion.1), channel_id=1, source_target_pairs={{8,0},{16,8},{24,16},{9,1},{17,9},{25,17},{10,2},{18,10},{26,18},{... | collective-permute-start | bytes 55304 | tf_op jit(solution)/shard_map/ppermute | solution.py:262
  492.1 5.8 %copy-start.40 = (bf16[2,2,2,2,2,48,4]{6,5,4,3,2,1,0:T(8,128)(2,1)S(1)}, bf16[2,2,2,2,2,48,4]{6,5,4,3,2,1,0:T(8,128)(2,1)}, u32[]{:S(2)}) copy-start(bf16[2,2,2,2,2,48,4]{6,5,4,3,2,1,0:T(8,128)(2,1)} %concatenate.80) | copy-start | bytes 36868
  502.5 69.7 %copy-start.67 = (f32[384]{0:T(512)S(1)}, f32[384]{0:T(512)}, u32[]{:S(2)}) copy-start(f32[384]{0:T(512)} %copy-done.66) | copy-start | bytes 4612
  (75 other events, 159.3 us)

commit v3 on v2

--- a/solution.py
+++ b/solution.py
@@ -19,6 +19,7 @@
 
 EPS = 1e-05
 MESH = pl.DeviceIdType.MESH
+ROWS_AT_ONCE = 16
 
 def tile(ref, base, lanes):
     return ref[pl.ds(pl.multiple_of(base, UNROLL), UNROLL), lanes]
@@ -483,6 +484,149 @@
     return jnp.dot(left, right, preferred_element_type=jnp.float32)
 
 
+def contract(left, right, left_dim, right_dim):
+    return lax.dot_general(left, right, (((left_dim,), (right_dim,)), ((), ())), preferred_element_type=jnp.float32)
+
+
+def expert_kernel(slices, *refs):
+    tokens_ref, grads_ref, column_ref, row_ref = refs[:4]
+    weights_in, weights_out = refs[4 : 4 + slices], refs[4 + slices : 4 + 2 * slices]
+    outs = refs[4 + 2 * slices :]
+    picked_ref, back_ref = outs[:2]
+    sums_in, sums_out = outs[2 : 2 + slices], outs[2 + slices : 2 + 2 * slices]
+    (sent, got, answer, returned, w_in, w_out, hidden, total, active, slope, inner,
+     send_sems, recv_sems, weight_sems, sum_sems) = outs[2 + 2 * slices :]
+    experts, room, width = sent.shape[1:]
+    places = experts * room
+    me = lax.axis_index("exp")
+    here = lax.axis_index("ctx")
+
+    loads = []
+    for s in range(slices):
+        loads.append(pltpu.make_async_copy(weights_in[s], w_in.at[s], weight_sems.at[0, s]))
+        loads.append(pltpu.make_async_copy(weights_out[s], w_out.at[s], weight_sems.at[1, s]))
+    for load in loads:
+        load.start()
+
+    barrier = pltpu.get_barrier_semaphore()
+    for step in range(1, experts):
+        pl.semaphore_signal(barrier, inc=1, device_id=(here, lax.rem(me + step, experts)), device_id_type=MESH)
+    pl.semaphore_wait(barrier, experts - 1)
+
+    def exchange(source, target, kind):
+        copies = []
+        for step in range(1, experts):
+            peer = lax.rem(me + step, experts)
+            copy = pltpu.make_async_remote_copy(
+                src_ref=source.at[peer],
+                dst_ref=target.at[me],
+                send_sem=send_sems.at[kind, step],
+                recv_sem=recv_sems.at[kind, step],
+                device_id=(here, peer),
+                device_id_type=MESH,
+            )
+            copy.start()
+            copies.append(copy)
+        target[me] = source[me]
+        return copies
+
+    def arrive(copies):
+        for copy in copies:
+            copy.wait_recv()
+
+    chooser = (lax.broadcasted_iota(jnp.int32, (places, row_ref.shape[1]), 0) == row_ref[...]).astype(jnp.float32).astype(jnp.bfloat16)
+    sent[0] = dot(chooser, tokens_ref[...]).astype(jnp.bfloat16).reshape(experts, room, width)
+    first = exchange(sent.at[0], got.at[0], 0)
+    sent[1] = dot(chooser, grads_ref[...]).astype(jnp.bfloat16).reshape(experts, room, width)
+    second = exchange(sent.at[1], got.at[1], 1)
+
+    for load in loads:
+        load.wait()
+    arrive(first)
+    rows = got[0].reshape(places, width)
+    for s in range(slices):
+        hidden[...] = dot(rows, w_in[s])
+
+        def curve(index, unused):
+            at = pl.ds(pl.multiple_of(index * ROWS_AT_ONCE, ROWS_AT_ONCE), ROWS_AT_ONCE)
+            value = hidden[at, :]
+            bell = 0.5 + 0.5 * lax.erf(value * 0.7071067811865476)
+            active[s, at, :] = (value * bell).astype(jnp.bfloat16)
+            slope[s, at, :] = bell + value * (jnp.exp(-0.5 * value * value) * 0.3989422804014327)
+            return unused
+
+        lax.fori_loop(0, places // ROWS_AT_ONCE, curve, 0)
+        product = dot(active[s], w_out[s])
+        total[...] = product if s == 0 else total[...] + product
+    answer[0] = total[...].astype(jnp.bfloat16).reshape(experts, room, width)
+    third = exchange(answer.at[0], returned.at[0], 2)
+
+    arrive(second)
+    pulled = got[1].reshape(places, width)
+    for s in range(slices):
+        inner[s] = (contract(pulled, w_out[s], 1, 1) * slope[s]).astype(jnp.bfloat16)
+        product = contract(inner[s], w_in[s], 1, 1)
+        total[...] = product if s == 0 else total[...] + product
+    answer[1] = total[...].astype(jnp.bfloat16).reshape(experts, room, width)
+    fourth = exchange(answer.at[1], returned.at[1], 3)
+
+    stores = []
+    for s in range(slices):
+        w_out[s] = contract(active[s], pulled, 0, 0).astype(jnp.bfloat16)
+        stores.append(pltpu.make_async_copy(w_out.at[s], sums_out[s], sum_sems.at[0, s]))
+        stores[-1].start()
+        w_in[s] = contract(rows, inner[s], 0, 0).astype(jnp.bfloat16)
+        stores.append(pltpu.make_async_copy(w_in.at[s], sums_in[s], sum_sems.at[1, s]))
+        stores[-1].start()
+
+    finder = (lax.broadcasted_iota(jnp.int32, (column_ref.shape[0], places), 1) == column_ref[...]).astype(jnp.float32).astype(jnp.bfloat16)
+    arrive(third)
+    picked_ref[...] = dot(finder, returned[0].reshape(places, width)).astype(jnp.bfloat16)
+    arrive(fourth)
+    back_ref[...] = dot(finder, returned[1].reshape(places, width)).astype(jnp.bfloat16)
+    for store in stores:
+        store.wait()
+    for copies in (first, second, third, fourth):
+        for copy in copies:
+            copy.wait_send()
+
+
+def run_experts(rows, grads, target, weights_in, weights_out, experts, room, identity):
+    slices = len(weights_in)
+    tokens, width = rows.shape
+    inner_width = weights_in[0].shape[1]
+    places = experts * room
+    inside = pl.BlockSpec(memory_space=pltpu.VMEM)
+    anywhere = pl.BlockSpec(memory_space=pl.ANY)
+    half = jnp.bfloat16
+    out = pl.pallas_call(
+        functools.partial(expert_kernel, slices),
+        in_specs=[inside] * 4 + [anywhere] * (2 * slices),
+        out_specs=[inside] * 2 + [anywhere] * (2 * slices),
+        out_shape=[jax.ShapeDtypeStruct(rows.shape, half)] * 2
+        + [jax.ShapeDtypeStruct(weight.shape, half) for weight in weights_in + weights_out],
+        scratch_shapes=[pltpu.VMEM((2, experts, room, width), half)] * 4
+        + [
+            pltpu.VMEM((slices, width, inner_width), half),
+            pltpu.VMEM((slices, inner_width, width), half),
+            pltpu.VMEM((places, inner_width), jnp.float32),
+            pltpu.VMEM((places, width), jnp.float32),
+            pltpu.VMEM((slices, places, inner_width), half),
+            pltpu.VMEM((slices, places, inner_width), jnp.float32),
+            pltpu.VMEM((slices, places, inner_width), half),
+            pltpu.SemaphoreType.DMA((4, experts)),
+            pltpu.SemaphoreType.DMA((4, experts)),
+            pltpu.SemaphoreType.DMA((2, slices)),
+            pltpu.SemaphoreType.DMA((2, slices)),
+        ],
+        compiler_params=pltpu.CompilerParams(
+            collective_id=identity, has_side_effects=True, vmem_limit_bytes=52 * 1024 * 1024
+        ),
+        name="run_experts",
+    )(rows, grads, target[:, None], target[None, :], *weights_in, *weights_out)
+    return out[0], out[1], list(out[2 : 2 + slices]), list(out[2 + slices :])
+
+
 def flipped(value, level):
     count = lax.axis_size("ctx")
     return lax.ppermute(value, "ctx", [(source, source ^ (1 << level)) for source in range(count)])
@@ -504,7 +648,7 @@
         kept = {}
         for offset in range(0, len(sums), 2 * step):
             arrived = flipped(sums[offset + step].astype(jnp.bfloat16), level)
-            kept[offset] = sums[offset] + arrived.astype(jnp.float32)
+            kept[offset] = sums[offset].astype(jnp.float32) + arrived.astype(jnp.float32)
         sums = [kept.get(offset) for offset in range(len(sums))]
     return sums[0]
 
@@ -548,6 +692,9 @@
     full_in, full_out, full_small = gather_all(
         sizes, (in_proj, out_proj, jnp.concatenate(columns, axis=1)), 0
     )
+    later_in, later_out, full_small = lax.optimization_barrier((expert_in[0], expert_out[0], full_small))
+    weights_in = spread_slices(later_in)
+    weights_out = spread_slices(later_out)
     full_xproj, full_dt, full_taps, full_bias, full_dtbias, full_decay, full_skip, gains, full_router = [
         full_small[:, end - width : end] for end, width in zip(ends, widths)
     ]
@@ -636,46 +783,18 @@
     gate_val = jnp.sum(probability * one_float, axis=1)
     running = jnp.cumsum(one_hot.astype(jnp.int32), axis=0)
     slot_index = jnp.sum(running * one_hot.astype(jnp.int32), axis=1) - 1
-    target = route_ids * capacity + slot_index
-    buffer = (
-        jnp.zeros((experts * capacity, D), jnp.bfloat16)
-        .at[target]
-        .set(normed_two)
-        .reshape(experts, capacity, D)
-    )
-    weights_in = spread_slices(expert_in[0])
-    weights_out = spread_slices(expert_out[0])
-    rows_in = lax.all_to_all(buffer, "exp", split_axis=0, concat_axis=0, tiled=True)
-    rows_in = rows_in.reshape(experts * capacity, D)
-    hidden_pre = [dot(rows_in, weight) for weight in weights_in]
-    active = [jax.nn.gelu(values, approximate=False).astype(jnp.bfloat16) for values in hidden_pre]
-    result = sum(dot(values, weight) for values, weight in zip(active, weights_out)).astype(jnp.bfloat16)
-    expert_result = result.reshape(experts, capacity, D)
-    returned = lax.all_to_all(expert_result, "exp", split_axis=0, concat_axis=0, tiled=True)
-    picked = returned.reshape(-1, D)[target].astype(jnp.float32)
+    room = -(-capacity // 16) * 16
+    target = route_ids * room + slot_index
+    grad_out = cotangent[0].astype(jnp.float32)
+    grad_pick = (grad_out * gate_val[:, None]).astype(jnp.bfloat16)
+    picked, grad_from_experts, grad_expert_in, grad_expert_out = run_experts(
+        normed_two, grad_pick, target, weights_in, weights_out, experts, room, 2
+    )
+    picked = picked.astype(jnp.float32)
+    grad_from_experts = grad_from_experts.astype(jnp.float32)
     outcome = residual + gate_val[:, None] * picked
     out_block = outcome.astype(jnp.bfloat16)[None]
-    grad_out = cotangent[0].astype(jnp.float32)
     grad_gate = jnp.sum(grad_out * picked, axis=1)
-    grad_pick = (grad_out * gate_val[:, None]).astype(jnp.bfloat16)
-    grad_buffer = (
-        jnp.zeros((experts * capacity, D), jnp.bfloat16)
-        .at[target]
-        .set(grad_pick)
-        .reshape(experts, capacity, D)
-    )
-    grad_result = lax.all_to_all(grad_buffer, "exp", split_axis=0, concat_axis=0, tiled=True)
-    grad_result = grad_result.reshape(experts * capacity, D)
-    grad_expert_out = [dot(values.T, grad_result) for values in active]
-    grad_hidden = []
-    for values, weight in zip(hidden_pre, weights_out):
-        gelu_value, gelu_pull = jax.vjp(lambda inner: jax.nn.gelu(inner, approximate=False), values)
-        grad_hidden.append(gelu_pull(dot(grad_result, weight.T))[0].astype(jnp.bfloat16))
-    grad_expert_in = [dot(rows_in.T, values) for values in grad_hidden]
-    grad_rows = sum(dot(values, weight.T) for values, weight in zip(grad_hidden, weights_in))
-    grad_rows = grad_rows.astype(jnp.bfloat16).reshape(experts, capacity, D)
-    grad_sent = lax.all_to_all(grad_rows, "exp", split_axis=0, concat_axis=0, tiled=True)
-    grad_from_experts = grad_sent.reshape(-1, D)[target].astype(jnp.float32)
     grad_w_in = collect_slices(grad_expert_in)[None]
     grad_w_out = collect_slices(grad_expert_out)[None]
     grad_probs = grad_gate[:, None] * one_float

time: 595 us -> 514 us (0.86)
  the two profiles are of different devices: /device:TPU:8 before, /device:TPU:0 now
where the time goes in v3:
time: 514 us; the launch traced here: 505 us
  Pallas kernels  269 us (52%)
  local copies, waits for them, and re-layouts  49.1 us (10%)
  matrix products  45.1 us (9%)
  other arithmetic  44.7 us (9%)
  waiting for transfers between devices  40.3 us (8%)
  starting transfers between devices  40.1 us (8%)
  blocking collectives  15 us (3%)
    pallas_call x1, Pallas kernels, run_experts(): pl.pallas_call(functools.partial(expert_kernel, slices), in_specs=[inside...  69.7 us
    pallas_call x1, Pallas kernels, reduce_all(): pl.pallas_call(functools.partial(reduce_kernel, places, streams, len(part...  68.5 us
    pallas_call x1, Pallas kernels, gather_all(): pl.pallas_call(functools.partial(gather_kernel, places, streams, len(shar...  60.3 us
    ppermute x12, waiting for transfers between devices, flipped(): lax.ppermute(value, 'ctx', [(source, source ^ 1 << level) for source in r...  40.3 us
    pallas_call x1, Pallas kernels, scan_adjoint(): pl.pallas_call(functools.partial(adjoint_kernel, pick(channels)), grid=(t...  34.7 us
    ppermute x3, starting transfers between devices, shifted(): lax.ppermute(value, axis, [(source, source + steps) for source in range(i...  34.2 us
    pallas_call x1, Pallas kernels, scan_out(): pl.pallas_call(functools.partial(out_kernel, pick(channels)), grid=(token...  17.9 us
    unnamed x142, local copies, waits for them, and re-layouts  12.4 us
  transfers between devices with their start and end apart: 15, of which 4 were waited for; matrix products, arithmetic and copies ran while one was open for 18% of the time, Pallas kernels for 19%

profile of v3, /device:TPU:0, one launch (start us, length us, event | category | flops | bytes accessed | tf_op | source)
XLA Modules:
  0.0 505.1 jit_solution(13104115605488767370)
XLA Ops:
  7.0 1.4 concatenate.66.refs_2_
  8.4 60.3 %gather_all.1 = (bf16[2,2,2,2,2,24,3072]{6,5,4,3,2,1,0:T(8,128)(2,1)}, bf16[2,2,2,2,2,48,768]{6,5,4,3,2,1,0:T(8,128)(2,1)}, bf16[2,2,2,2,2,48,156]{6,5,4,3,2,1,0:T(8,128)(2,1)}) custom-call(bf16[24,3072]{1,0:T(8,128)(2,1)} %refs_0_.1, bf16[48,768]{1,0:T(8,128)(2,1)} %refs_1_.1, bf16[48,156]{1,0:T(8,128)(2,1)} %concatenate.66.refs_2_), custom_call_target="tpu_custom_call" | custom-call | tf_op jit(solution)/shard_map/gather_all/pallas_call | solution.py:374
  69.4 1.5 collective-permute-start.6
  71.7 2.3 collective-permute-start
  74.1 1.3 slice_reduce_fusion.4
  75.7 1.3 fusion.23
  77.5 6.8 %fusion.100 = (bf16[384,3072]{1,0:T(8,128)(2,1)S(1)}, f32[384,3072]{1,0:T(8,128)}) fusion(bf16[768,3072]{1,0:T(8,128)(2,1)} %bitcast.198, bf16[1,384,768]{2,1,0:T(8,128)(2,1)} %param.18, f32[768]{0:T(1024)S(1)} %reshape.366, f32[384]{0:T(512)S(1)} %fusion.81), kind=kOutput, calls=%fused_computation.208 | convolution fusion | flops 1814298624 | bytes 12390912 | tf_op jit(solution)/shard_map/dot_general | solution.py:713
  89.2 1.5 slice_reduce_fusion.3
  91.9 30.3 %collective-permute-start.1 = (bf16[3,1536]{1,0:T(4,128)(2,1)S(1)}, bf16[3,1536]{1,0:T(4,128)(2,1)S(1)}, u32[]{:S(2)}, u32[]{:S(2)}) collective-permute-start(bf16[3,1536]{1,0:T(4,128)(2,1)S(1)} %slice.266), channel_id=1, source_target_pairs={{0,8},{8,16},{16,24},{1,9},{9,17},{17,25},{2,10},{10,18},{18,26},{... | collective-permute-start | bytes 27656 | tf_op jit(solution)/shard_map/ppermute | solution.py:263
  124.0 3.2 multiply_convert_fusion.1
  128.5 4.1 fusion.96
  134.6 3.1 broadcast_in_dim.57.b_ref
  137.8 8.6 %shard_map.297 = f32[16,1536]{1,0:T(8,128)S(1)} custom-call(f32[384,1536]{1,0:T(8,128)S(1)} %get-tuple-element.178.step_ref, f32[384,1536]{1,0:T(8,128)S(1)} %copy-done.1, f32[384,16,128]{2,1,0:T(8,128)} %broadcast_in_dim.57.b_ref, f32[16,1536]{1,0:T(8,128)S(1)} %get-tuple-element.192.rate_ref), custom_call_target="tpu_custom_call" | custom-call | tf_op jit(solution)/shard_map/pallas_call | solution.py:200
  146.4 9.4 %all_gather.6 = bf16[4,2,16,1536]{3,2,1,0:T(8,128)(2,1)S(1)} all-gather(bf16[1,2,16,1536]{3,2,1,0:T(8,128)(2,1)S(1)} %pad_maximum_fusion.3), channel_id=1, replica_groups=mesh['ctx'=4,'exp'=8] {'ctx'}, dimensions={0}, use_global_device_ids=true | all-gather | bytes 491520 | tf_op jit(solution)/shard_map/all_gather | solution.py:751
  156.8 1.5 copy.145
  158.3 3.0 broadcast_in_dim.58.c_ref
  161.3 17.9 %shard_map.298 = (f32[384,1536]{1,0:T(8,128)S(1)}, bf16[384,16,1536]{2,1,0:T(8,128)(2,1)}, bf16[6,16,1536]{2,1,0:T(8,128)(2,1)S(1)}) custom-call(f32[384,1536]{1,0:T(8,128)S(1)} %get-tuple-element.178.step_ref, f32[384,1536]{1,0:T(8,128)} %get-tuple-element.186.push_ref, f32[384,16,128]{2,1,0:T(8,128)} %broadcast_in_dim.57.b_ref, ...), custom_call_target="tpu_custom_call" | custom-call | tf_op jit(solution)/shard_map/pallas_call | solution.py:215
  179.2 2.6 multiply_convert_fusion
  186.2 1.8 collective-permute-done.7.refs_11_
  188.0 69.7 %run_experts.1 = (bf16[384,768]{1,0:T(8,128)(2,1)S(1)}, bf16[384,768]{1,0:T(8,128)(2,1)S(1)}, bf16[768,768]{1,0:T(8,128)(2,1)}, bf16[768,768]{1,0:T(8,128)(2,1)}...) custom-call(bf16[384,768]{1,0:T(8,128)(2,1)S(1)} %multiply_convert_f, ...), custom_call_target="tpu_custom_call" | custom-call | tf_op jit(solution)/shard_map/run_experts/pallas_call | solution.py:602
  259.9 1.3 convert_add_fusion
  261.8 5.6 %fusion.8 = (bf16[1536]{0:T(1024)(128)(2,1)}, f32[384,1536]{1,0:T(8,128)S(1)}, bf16[384,1536]{1,0:T(8,128)(2,1)}) fusion(bf16[384,1536]{1,0:T(8,128)(2,1)S(1)} %copy-done.9, f32[384,3072]{1,0:T(8,128)} %get-tuple-element.202, f32[384,1536]{1,0:T(8,128)S(1)} %get-tuple-element.46, f32[1536]{0:T(1024)S(1)} %copy-done.35, bf16[1536,768]{1,0:T(8,128)(2,1)S(1)} %bitcast.201, ...), kind=kOutput, calls=%fused_computation.20 | convolution fusion | flops 916879872 | bytes 12985344 | tf_op jit(solution)/shard_map/dot_general | solution.py:811
  267.4 9.1 %shard_map.299 = f32[16,1536]{1,0:T(8,128)S(1)} custom-call(f32[384,1536]{1,0:T(8,128)S(1)} %get-tuple-element.178.step_ref, f32[384,1536]{1,0:T(8,128)S(1)} %get-tuple-element.174.grad_ref, f32[384,16,128]{2,1,0:T(8,128)} %broadcast_in_dim.58.c_ref, f32[16,1536]{1,0:T(8,128)S(1)} %get-tuple-element.192.rate_ref), custom_call_target="tpu_custom_call" | custom-call | tf_op jit(solution)/shard_map/pallas_call | solution.py:230
  276.5 5.6 %all-gather = bf16[64,1536]{1,0:T(8,128)(2,1)S(1)} all-gather(bf16[16,1536]{1,0:T(8,128)(2,1)S(1)} %convert_element_type.251), channel_id=2, replica_groups=mesh['ctx'=4,'exp'=8] {'ctx'}, dimensions={0}, use_global_device_ids=true | all-gather | bytes 245760 | tf_op jit(solution)/shard_map/all_gather | solution.py:816
  282.2 34.7 %shard_map.300 = (f32[384,1536]{1,0:T(8,128)S(1)}, f32[384,1536]{1,0:T(8,128)S(1)}, f32[384,16,128]{2,1,0:T(8,128)}, f32[384,16,128]{2,1,0:T(8,128)}, f32[16,1536]{1,0:T(8,128)S(1)}) custom-call(f32[384,1536]{1,0:T(8,128)} %copy-done, f32[384,1536]{1,0:T(8,128)} %get-tuple-element.186.push_ref, f32[384,1536]{1,0:T(8,128)} %copy-done.2, ...), custom_call_target="tpu_custom_call" | custom-call | tf_op jit(solution)/shard_map/pallas_call | solution.py:246
  317.0 1.6 fusion.94
  320.3 2.8 reduce_sum.198
  323.2 2.9 reduce_sum.202
  326.3 9.4 %multiply_reduce_fusion.3 = (f32[1536]{0:T(1024)S(1)}, f32[1536]{0:T(1024)S(1)}, f32[1536]{0:T(1024)S(1)}, f32[1536]{0:T(1024)S(1)}, bf16[1536]{0:T(1024)(128)(2...) fusion(f32[387,1536]{1,0:T(8,128)} %copy-done.7, ...), kind=kOutput, calls=%fused_computation.31 | convolution fusion | flops 115192320 | bytes 28840960 | tf_op jit(solution)/shard_map/dot_general | solution.py:851
  335.8 2.6 pad_add_fusion
  340.0 1.4 convolution_convert_fusion.1
  342.6 1.5 collective-permute-start.8
  349.2 1.4 concatenate.82
  351.5 1.5 concatenate.83
  353.0 1.5 concatenate.84
  354.5 2.0 fusion.9
  356.6 5.8 %fusion.20 = (bf16[768]{0:T(1024)(128)(2,1)S(1)}, f32[384]{0:T(512)S(1)}, f32[384,768]{1,0:T(8,128)}) fusion(bf16[1,384,768]{2,1,0:T(8,128)(2,1)S(1)} %copy-done.21, f32[384]{0:T(512)S(1)} %copy-done.59, f32[768]{0:T(1024)S(1)} %copy-done.49, bf16[768,3072]{1,0:T(8,128)(2,1)} %bitcast.199, bf16[384,1536]{1,0:T(8,128)(2,1)S(1)} %copy-done.65, ...), kind=kOutput, calls=%fused_computation.61 | convolution fusion | flops 1818721152 | bytes 8855040 | tf_op jit(solution)/shard_map/dot_general | solution.py:861
  363.6 4.6 concatenate.81.refs_2_
  368.2 6.7 %convolution_convert_fusion = bf16[768,3072]{1,0:T(8,128)(2,1)} fusion(bf16[384,1536]{1,0:T(8,128)(2,1)} %get-tuple-element.181, bf16[384,1536]{1,0:T(8,128)(2,1)} %copy-done.27, bf16[1,384,768]{2,1,0:T(8,128)(2,1)} %param.18, f32[384]{0:T(512)S(1)} %copy-done.59, f32[768]{0:T(1024)S(1)} %copy-done.49), kind=kOutput, calls=%fused_computation.1 | convolution fusion | flops 1820196864 | bytes 7672320 | tf_op jit(solution)/shard_map/dot_general | solution.py:860
  374.9 68.5 %reduce_all.1 = (f32[24,3072]{1,0:T(8,128)S(1)}, f32[48,768]{1,0:T(8,128)S(1)}, f32[48,156]{1,0:T(8,128)S(1)}) custom-call(bf16[2,2,2,2,2,24,3072]{6,5,4,3,2,1,0:T(8,128)(2,1)} %bitcast.181, bf16[2,2,2,2,2,48,768]{6,5,4,3,2,1,0:T(8,128)(2,1)S(1)} %bitcast.172, bf16[2,2,2,2,2,48,156]{6,5,4,3,2,1,0:T(8,128)(2,1)S(1)} %concatenate.81.refs_2_), custom_call_target="tpu_custom_call" | custom-call | tf_op jit(solution)/shard_map/reduce_all/pallas_call | solution.py:466
  443.5 2.7 add_convert_fusion
  446.6 2.7 add_convert_fusion.1
  449.2 1.5 collective-permute-start.11
  455.7 2.6 fusion.28
  458.3 17.0 %collective-permute-done.14 = bf16[768,768]{1,0:T(8,128)(2,1)} collective-permute-done((bf16[768,768]{1,0:T(8,128)(2,1)}, bf16[768,768]{1,0:T(8,128)(2,1)}, u32[]{:S(2)}, u32[]{:S(2)}) %collective-permute-start.14) | collective-permute-done | bytes 1179680 | tf_op jit(solution)/shard_map/ppermute | solution.py:632
  475.3 3.9 add_bitcast_fusion
  479.2 20.5 %collective-permute-done.11 = bf16[768,768]{1,0:T(8,128)(2,1)} collective-permute-done((bf16[768,768]{1,0:T(8,128)(2,1)}, bf16[768,768]{1,0:T(8,128)(2,1)}, u32[]{:S(2)}, u32[]{:S(2)}) %collective-permute-start.11) | collective-permute-done | bytes 1179680 | tf_op jit(solution)/shard_map/ppermute | solution.py:632
  499.7 3.6 add_bitcast_fusion.1
  (254 shorter events, 46.2 us)
Async XLA Ops:
  68.7 114.4 %collective-permute-start.3 = (bf16[768,768]{1,0:T(8,128)(2,1)}, bf16[768,768]{1,0:T(8,128)(2,1)}, u32[]{:S(2)}, u32[]{:S(2)}) collective-permute-start(bf16[768,768]{1,0:T(8,128)(2,1)} %bitcast.186), channel_id=1, source_target_pairs={{0,16},{8,24},{16,0},{24,8},{1,17},{9,25},{17,1},{25,9},{2,18},{10... | collective-permute-start | bytes 3538952 | tf_op jit(solution)/shard_map/ppermute | solution.py:632
  69.3 115.9 %collective-permute-start.2 = (bf16[768,768]{1,0:T(8,128)(2,1)}, bf16[768,768]{1,0:T(8,128)(2,1)}, u32[]{:S(2)}, u32[]{:S(2)}) collective-permute-start(bf16[768,768]{1,0:T(8,128)(2,1)} %bitcast.187), channel_id=1, source_target_pairs={{0,8},{8,0},{16,24},{24,16},{1,9},{9,1},{17,25},{25,17},{2,10},{10... | collective-permute-start | bytes 3538952 | tf_op jit(solution)/shard_map/ppermute | solution.py:632
  69.4 114.0 %collective-permute-start.6 = (bf16[768,768]{1,0:T(8,128)(2,1)}, bf16[768,768]{1,0:T(8,128)(2,1)}, u32[]{:S(2)}, u32[]{:S(2)}) collective-permute-start(bf16[768,768]{1,0:T(8,128)(2,1)} %bitcast.189), channel_id=1, source_target_pairs={{0,16},{8,24},{16,0},{24,8},{1,17},{9,25},{17,1},{25,9},{2,18},{10... | collective-permute-start | bytes 3538952 | tf_op jit(solution)/shard_map/ppermute | solution.py:632
  70.9 114.2 %collective-permute-start.5 = (bf16[768,768]{1,0:T(8,128)(2,1)}, bf16[768,768]{1,0:T(8,128)(2,1)}, u32[]{:S(2)}, u32[]{:S(2)}) collective-permute-start(bf16[768,768]{1,0:T(8,128)(2,1)} %bitcast.190), channel_id=1, source_target_pairs={{0,8},{8,0},{16,24},{24,16},{1,9},{9,1},{17,25},{25,17},{2,10},{10... | collective-permute-start | bytes 3538952 | tf_op jit(solution)/shard_map/ppermute | solution.py:632
  71.7 20.1 %collective-permute-start = (bf16[3]{0:T(256)(128)(2,1)S(1)}, bf16[3]{0:T(256)(128)(2,1)S(1)}, u32[]{:S(2)}, u32[]{:S(2)}) collective-permute-start(bf16[3]{0:T(256)(128)(2,1)S(1)} %fusion.83), channel_id=1, source_target_pairs={{0,8},{8,16},{16,24},{1,9},{9,17},{17,25},{2,10},{10,18},{18,26},{... | collective-permute-start | bytes 26 | tf_op jit(solution)/shard_map/ppermute | solution.py:263
  75.7 8.7 %copy-start.48 = (f32[768]{0:T(1024)}, f32[768]{0:T(1024)S(1)}, u32[]{:S(2)}) copy-start(f32[768]{0:T(1024)S(1)} %reshape.366) | copy-start | bytes 9220
  77.0 7.4 %copy-start.58 = (f32[384]{0:T(512)}, f32[384]{0:T(512)S(1)}, u32[]{:S(2)}) copy-start(f32[384]{0:T(512)S(1)} %fusion.81) | copy-start | bytes 4612
  90.7 36.5 %copy-start.37 = (f32[1536]{0:T(1024)}, f32[1536]{0:T(1024)S(1)}, u32[]{:S(2)}) copy-start(f32[1536]{0:T(1024)S(1)} %get-tuple-element.162) | copy-start | bytes 18436
  90.7 36.5 %copy-start.39 = (f32[1536]{0:T(1024)}, f32[1536]{0:T(1024)S(1)}, u32[]{:S(2)}) copy-start(f32[1536]{0:T(1024)S(1)} %get-tuple-element.163) | copy-start | bytes 18436
  90.7 36.5 %copy-start.41 = (f32[1536]{0:T(1024)}, f32[1536]{0:T(1024)S(1)}, u32[]{:S(2)}) copy-start(f32[1536]{0:T(1024)S(1)} %get-tuple-element.164) | copy-start | bytes 18436
  90.7 36.5 %copy-start.43 = (f32[1536]{0:T(1024)}, f32[1536]{0:T(1024)S(1)}, u32[]{:S(2)}) copy-start(f32[1536]{0:T(1024)S(1)} %get-tuple-element.165) | copy-start | bytes 18436
  91.9 31.8 %collective-permute-start.1 = (bf16[3,1536]{1,0:T(4,128)(2,1)S(1)}, bf16[3,1536]{1,0:T(4,128)(2,1)S(1)}, u32[]{:S(2)}, u32[]{:S(2)}) collective-permute-start(bf16[3,1536]{1,0:T(4,128)(2,1)S(1)} %slice.266), channel_id=1, source_target_pairs={{0,8},{8,16},{16,24},{1,9},{9,17},{17,25},{2,10},{10,18},{18,26},{... | collective-permute-start | bytes 27656 | tf_op jit(solution)/shard_map/ppermute | solution.py:263
  123.6 3.7 copy-start.55
  127.3 5.3 %copy-start.8 = (bf16[384,1536]{1,0:T(8,128)(2,1)}, bf16[384,1536]{1,0:T(8,128)(2,1)S(1)}, u32[]{:S(2)}) copy-start(bf16[384,1536]{1,0:T(8,128)(2,1)S(1)} %get-tuple-element.179) | copy-start | bytes 3538948
  127.8 4.8 copy-start.32
  132.6 134.8 %copy-start = (f32[384,1536]{1,0:T(8,128)}, f32[384,1536]{1,0:T(8,128)S(1)}, u32[]{:S(2)}) copy-start(f32[384,1536]{1,0:T(8,128)S(1)} %get-tuple-element.178.step_ref) | copy-start | bytes 7077892
  133.6 4.2 copy-start.1
  161.3 17.9 %copy-start.9 = (bf16[384,1536]{1,0:T(8,128)(2,1)S(1)}, bf16[384,1536]{1,0:T(8,128)(2,1)}, u32[]{:S(2)}) copy-start(bf16[384,1536]{1,0:T(8,128)(2,1)} %copy-done.8) | copy-start | bytes 3538948
  161.3 17.9 %copy-start.35 = (f32[1536]{0:T(1024)S(1)}, f32[1536]{0:T(1024)}, u32[]{:S(2)}) copy-start(f32[1536]{0:T(1024)} %get-tuple-element.159) | copy-start | bytes 18436
  183.0 3.1 collective-permute-start.4
  183.5 4.5 collective-permute-start.7
  261.2 6.2 %copy-start.17 = (f32[384,768]{1,0:T(8,128)}, f32[384,768]{1,0:T(8,128)S(1)}, u32[]{:S(2)}) copy-start(f32[384,768]{1,0:T(8,128)S(1)} %get-tuple-element.187) | copy-start | bytes 3538948
  267.4 9.1 %copy-start.2 = (f32[384,1536]{1,0:T(8,128)}, f32[384,1536]{1,0:T(8,128)S(1)}, u32[]{:S(2)}) copy-start(f32[384,1536]{1,0:T(8,128)S(1)} %get-tuple-element.174.grad_ref) | copy-start | bytes 7077892
  267.4 14.8 %copy-start.16 = (f32[4,2,16,1536]{3,2,1,0:T(8,128)S(1)}, f32[4,2,16,1536]{3,2,1,0:T(8,128)}, u32[]{:S(2)}) copy-start(f32[4,2,16,1536]{3,2,1,0:T(8,128)} %copy-done.15) | copy-start | bytes 2359300
  282.2 34.8 %copy-start.23 = (f32[384,1536]{1,0:T(8,128)S(1)}, f32[384,1536]{1,0:T(8,128)}, u32[]{:S(2)}) copy-start(f32[384,1536]{1,0:T(8,128)} %get-tuple-element.203) | copy-start | bytes 7077892
  340.0 5.1 %copy-start.34 = (bf16[768,8]{0,1:T(8,128)(2,1)S(1)}, bf16[768,8]{0,1:T(8,128)(2,1)}, u32[]{:S(2)}) copy-start(bf16[768,8]{0,1:T(8,128)(2,1)} %convolution_convert_fusion.5) | copy-start | bytes 36868
  340.0 6.2 %copy-start.57 = (bf16[768]{0:T(1024)(128)(2,1)S(1)}, bf16[768]{0:T(1024)(128)(2,1)}, u32[]{:S(2)}) copy-start(bf16[768]{0:T(1024)(128)(2,1)} %get-tuple-element.154) | copy-start | bytes 4612
  341.4 7.7 %copy-start.62 = (bf16[1536]{0:T(1024)(128)(2,1)S(1)}, bf16[1536]{0:T(1024)(128)(2,1)}, u32[]{:S(2)}) copy-start(bf16[1536]{0:T(1024)(128)(2,1)} %get-tuple-element.156) | copy-start | bytes 9220
  341.5 10.1 %copy-start.47 = (bf16[1536]{0:T(1024)(128)(2,1)S(1)}, bf16[1536]{0:T(1024)(128)(2,1)}, u32[]{:S(2)}) copy-start(bf16[1536]{0:T(1024)(128)(2,1)} %get-tuple-element.175) | copy-start | bytes 9220
  341.5 11.5 %copy-start.61 = (bf16[1536]{0:T(1024)(128)(2,1)S(1)}, bf16[1536]{0:T(1024)(128)(2,1)}, u32[]{:S(2)}) copy-start(bf16[1536]{0:T(1024)(128)(2,1)} %get-tuple-element.173) | copy-start | bytes 9220
  341.5 102.0 %collective-permute-start.13 = (bf16[768,768]{1,0:T(8,128)(2,1)}, bf16[768,768]{1,0:T(8,128)(2,1)}, u32[]{:S(2)}, u32[]{:S(2)}) collective-permute-start(bf16[768,768]{1,0:T(8,128)(2,1)} %get-tuple-element.69), channel_id=1, source_target_pairs={{0,8},{8,0},{16,24},{24,16},{1,9},{9,1},{17,25},{25,17},{2,10},{10... | collective-permute-start | bytes 3538952 | tf_op jit(solution)/shard_map/ppermute | solution.py:632
  341.9 116.4 %collective-permute-start.12 = (bf16[768,768]{1,0:T(8,128)(2,1)}, bf16[768,768]{1,0:T(8,128)(2,1)}, u32[]{:S(2)}, u32[]{:S(2)}) collective-permute-start(bf16[768,768]{1,0:T(8,128)(2,1)} %get-tuple-element.67), channel_id=1, source_target_pairs={{0,8},{8,0},{16,24},{24,16},{1,9},{9,1},{17,25},{25,17},{2,10},{10... | collective-permute-start | bytes 3538952 | tf_op jit(solution)/shard_map/ppermute | solution.py:632
  342.1 104.5 %collective-permute-start.10 = (bf16[768,768]{1,0:T(8,128)(2,1)}, bf16[768,768]{1,0:T(8,128)(2,1)}, u32[]{:S(2)}, u32[]{:S(2)}) collective-permute-start(bf16[768,768]{1,0:T(8,128)(2,1)} %get-tuple-element.65), channel_id=1, source_target_pairs={{0,8},{8,0},{16,24},{24,16},{1,9},{9,1},{17,25},{25,17},{2,10},{10... | collective-permute-start | bytes 3538952 | tf_op jit(solution)/shard_map/ppermute | solution.py:632
  342.4 136.8 %collective-permute-start.9 = (bf16[768,768]{1,0:T(8,128)(2,1)}, bf16[768,768]{1,0:T(8,128)(2,1)}, u32[]{:S(2)}, u32[]{:S(2)}) collective-permute-start(bf16[768,768]{1,0:T(8,128)(2,1)} %get-tuple-element.63), channel_id=1, source_target_pairs={{0,8},{8,0},{16,24},{24,16},{1,9},{9,1},{17,25},{25,17},{2,10},{10... | collective-permute-start | bytes 3538952 | tf_op jit(solution)/shard_map/ppermute | solution.py:632
  342.6 11.9 %collective-permute-start.8 = (f32[3,1536]{1,0:T(4,128)S(1)}, f32[3,1536]{1,0:T(4,128)S(1)}, u32[]{:S(2)}, u32[]{:S(2)}) collective-permute-start(f32[3,1536]{1,0:T(4,128)S(1)} %pad_add_fusion.1), channel_id=1, source_target_pairs={{8,0},{16,8},{24,16},{9,1},{17,9},{25,17},{10,2},{18,10},{26,18},{... | collective-permute-start | bytes 55304 | tf_op jit(solution)/shard_map/ppermute | solution.py:263
  350.6 5.9 %copy-start.21 = (bf16[1,384,768]{2,1,0:T(8,128)(2,1)S(1)}, bf16[1,384,768]{2,1,0:T(8,128)(2,1)}, u32[]{:S(2)}) copy-start(bf16[1,384,768]{2,1,0:T(8,128)(2,1)} %param.18) | copy-start | bytes 1769476
  350.6 5.9 %copy-start.49 = (f32[768]{0:T(1024)S(1)}, f32[768]{0:T(1024)}, u32[]{:S(2)}) copy-start(f32[768]{0:T(1024)} %copy-done.48) | copy-start | bytes 9220
  350.6 5.9 %copy-start.59 = (f32[384]{0:T(512)S(1)}, f32[384]{0:T(512)}, u32[]{:S(2)}) copy-start(f32[384]{0:T(512)} %copy-done.58) | copy-start | bytes 4612
  356.5 5.9 %copy-start.27 = (bf16[384,1536]{1,0:T(8,128)(2,1)}, bf16[384,1536]{1,0:T(8,128)(2,1)S(1)}, u32[]{:S(2)}) copy-start(bf16[384,1536]{1,0:T(8,128)(2,1)S(1)} %fusion.9) | copy-start | bytes 3538948
  374.9 68.6 %copy-start.26 = (bf16[768,768]{1,0:T(8,128)(2,1)S(1)}, bf16[768,768]{1,0:T(8,128)(2,1)}, u32[]{:S(2)}) copy-start(bf16[768,768]{1,0:T(8,128)(2,1)} %get-tuple-element.68) | copy-start | bytes 3538948
  443.4 5.9 %copy-start.5 = (f32[48,768]{1,0:T(8,128)}, f32[48,768]{1,0:T(8,128)S(1)}, u32[]{:S(2)}) copy-start(f32[48,768]{1,0:T(8,128)S(1)} %get-tuple-element.239) | copy-start | bytes 442372
  446.1 9.5 %copy-start.46 = (f32[384]{0:T(512)S(1)}, f32[384]{0:T(512)}, u32[]{:S(2)}) copy-start(f32[384]{0:T(512)} %copy-done.45) | copy-start | bytes 4612
  446.1 9.6 %copy-start.19 = (f32[384,768]{1,0:T(8,128)S(1)}, f32[384,768]{1,0:T(8,128)}, u32[]{:S(2)}) copy-start(f32[384,768]{1,0:T(8,128)} %copy-done.17) | copy-start | bytes 3538948
  446.2 9.6 %copy-start.22 = (bf16[1,384,768]{2,1,0:T(8,128)(2,1)S(1)}, bf16[1,384,768]{2,1,0:T(8,128)(2,1)}, u32[]{:S(2)}) copy-start(bf16[1,384,768]{2,1,0:T(8,128)(2,1)} %param.18) | copy-start | bytes 1769476
  446.2 29.1 %collective-permute-start.14 = (bf16[768,768]{1,0:T(8,128)(2,1)}, bf16[768,768]{1,0:T(8,128)(2,1)}, u32[]{:S(2)}, u32[]{:S(2)}) collective-permute-start(bf16[768,768]{1,0:T(8,128)(2,1)} %add_convert_fusion), channel_id=1, source_target_pairs={{0,16},{8,24},{16,0},{24,8},{1,17},{9,25},{17,1},{25,9},{2,18},{10... | collective-permute-start | bytes 3538952 | tf_op jit(solution)/shard_map/ppermute | solution.py:632
  449.2 50.4 %collective-permute-start.11 = (bf16[768,768]{1,0:T(8,128)(2,1)}, bf16[768,768]{1,0:T(8,128)(2,1)}, u32[]{:S(2)}, u32[]{:S(2)}) collective-permute-start(bf16[768,768]{1,0:T(8,128)(2,1)} %add_convert_fusion.1), channel_id=1, source_target_pairs={{0,16},{8,24},{16,0},{24,8},{1,17},{9,25},{17,1},{25,9},{2,18},{10... | collective-permute-start | bytes 3538952 | tf_op jit(solution)/shard_map/ppermute | solution.py:632
  475.3 24.4 %copy-start.28 = (bf16[768,768]{1,0:T(8,128)(2,1)S(1)}, bf16[768,768]{1,0:T(8,128)(2,1)}, u32[]{:S(2)}) copy-start(bf16[768,768]{1,0:T(8,128)(2,1)} %get-tuple-element.62) | copy-start | bytes 3538948
  499.7 4.3 copy-start.6
  (33 other events, 78.2 us)
